TPU v7x, 32 devices: a whole 2x2x4 slice. The times are simulated.
32 devices in a mesh: dom: 4 (over y, core), cls: 8 (over z, x).
Axes of the slice: x: 2, y: 2, z: 4, core: 2. Of those that a mesh axis runs over, the one named last changes fastest.
Arguments:
- particles: bfloat16 [1536, 64, 288], P(('dom', 'cls')), may hold values from -6 to 6
- references: bfloat16 [200, 64, 288], P('cls'), may hold values from -6 to 6
- class_block: int32 [1536, 1], P(('dom', 'cls')), may hold values from 0 to 7; in each aligned block of 48 rows (0 to 47, 48 to 95, ...) at most 12 rows name the same one
- class_local: int32 [1536], P(('dom', 'cls')), may hold values from 0 to 24
- rotation: int32 [1536], P(('dom', 'cls')), may hold values from 0 to 35
- shifts: int32 [1536, 2], P(('dom', 'cls')), may hold values from -5 to 5
- defocus: int32 [1536], P(('dom', 'cls')), may hold values from 0 to 15
Outputs:
- best_score: float32 [1536], P(('dom', 'cls'))
- class_average: float32 [200, 64, 288], P('cls', 'dom')
Inputs may be any that keep to these rules, and one draw needn't show every extreme that they name: `class_block`: in the rows of one device no class block is named more than 12 times, and some class block is named exactly 12 times by some device.
All inputs are finite; a program needn't handle non-finite values.
Results may differ from a plain program's by a relative error of at most 0.0045.
Values may be sent and summed in bfloat16 or wider, within the bound.
A program may use at most 128 MiB of HBM per device.

v0:
```python
import math

import jax
import jax.numpy as jnp
from jax import lax
from jax.sharding import PartitionSpec as P

ROT = 36
BOX = 128
NBINS = 16


EPSILON = 1e-06


def angle_table(angles):
    sample_index = jnp.arange(angles, dtype=jnp.int32)
    turn_count = sample_index[:, None] * sample_index[None, :] % angles
    angle_value = turn_count.astype(jnp.float32) * (2.0 * math.pi / angles)
    cosine = jnp.cos(angle_value)
    sine_part = jnp.sin(angle_value)
    upper_half = jnp.concatenate([cosine, -sine_part], axis=1)
    lower_half = jnp.concatenate([sine_part, cosine], axis=1)
    return jnp.concatenate([upper_half, lower_half], axis=0).astype(jnp.bfloat16)


def rotation_table(angles, rotations):
    rotate_step = angles // rotations
    harmonic = jnp.arange(angles, dtype=jnp.int32)
    rotate_index = jnp.arange(rotations, dtype=jnp.int32)
    turn_count = harmonic[:, None] * (rotate_step * rotate_index[None, :]) % angles
    angle_value = turn_count.astype(jnp.float32) * (2.0 * math.pi / angles)
    return jnp.stack([jnp.cos(angle_value), jnp.sin(angle_value)]) * (1.0 / angles)


def ctf_table(bins, cycle_count):
    radius = (jnp.arange(cycle_count, dtype=jnp.int32) + 1).astype(jnp.float32) / cycle_count
    defocus_level = jnp.arange(bins, dtype=jnp.int32).astype(jnp.float32) / bins
    phase = math.pi * (3.0 + 9.0 * defocus_level[:, None]) * (radius[None, :] * radius[None, :])
    return 0.995 * jnp.sin(phase) + 0.1 * jnp.cos(phase)


def ctf_rows(defocus, bins, cycle_count):
    defocus_hits = (defocus[:, None] == jnp.arange(bins, dtype=jnp.int32)[None, :]).astype(
        jnp.float32
    )
    return jnp.dot(defocus_hits, ctf_table(bins, cycle_count), precision=lax.Precision.HIGHEST)


def shift_phase(shifts, cycle_count, angles):
    angle_value = jnp.arange(angles, dtype=jnp.int32).astype(jnp.float32) * (2.0 * math.pi / angles)
    radius = jnp.arange(cycle_count, dtype=jnp.int32).astype(jnp.float32)
    shift_x = shifts[:, 0].astype(jnp.float32)
    shift_y = shifts[:, 1].astype(jnp.float32)
    along_beam = (
        shift_x[:, None] * jnp.cos(angle_value)[None, :]
        + shift_y[:, None] * jnp.sin(angle_value)[None, :]
    )
    return 2.0 * math.pi / BOX * radius[None, :, None] * along_beam[:, None, :]


def prepare(particles, rotation, shifts, defocus):
    particle_count, cycle_count, row_width = particles.shape
    angles = row_width // 2
    phase = shift_phase(shifts, cycle_count, angles)
    real_part = particles[:, :, :angles].astype(jnp.float32)
    imag_part = particles[:, :, angles:].astype(jnp.float32)
    cos_phase = jnp.cos(phase)
    sin_phase = jnp.sin(phase)
    shifted = jnp.concatenate(
        [
            real_part * cos_phase - imag_part * sin_phase,
            real_part * sin_phase + imag_part * cos_phase,
        ],
        axis=2,
    ).astype(jnp.bfloat16)
    spectrum = jnp.dot(
        shifted.reshape(particle_count * cycle_count, row_width),
        angle_table(angles),
        preferred_element_type=jnp.float32,
    ).reshape(particle_count, cycle_count, row_width)
    contrast = ctf_rows(defocus, NBINS, cycle_count)
    weighted = (contrast[:, :, None] * spectrum).astype(jnp.bfloat16)
    rotate_step = angles // ROT
    harmonic = jnp.arange(angles, dtype=jnp.int32)
    turn_count = harmonic[None, :] * (rotate_step * rotation[:, None]) % angles
    angle_value = turn_count.astype(jnp.float32) * (2.0 * math.pi / angles)
    cos_rot = jnp.cos(angle_value)[:, None, :]
    sin_rot = jnp.sin(angle_value)[:, None, :]
    spec_real = spectrum[:, :, :angles]
    spec_imag = spectrum[:, :, angles:]
    turned = jnp.concatenate(
        [spec_real * cos_rot - spec_imag * sin_rot, spec_real * sin_rot + spec_imag * cos_rot],
        axis=2,
    )
    unrotated = (contrast[:, :, None] * turned).astype(jnp.bfloat16)
    return (contrast, weighted, unrotated)


def block_scores(stacked_major, contrast, harmonics, rotate_table):
    angles = stacked_major.shape[0]
    class_count = harmonics.shape[0]
    harm_real = harmonics[:, :, :angles]
    harm_imag = harmonics[:, :, angles:]
    paired = jnp.concatenate(
        [
            jnp.concatenate([harm_real, harm_imag], axis=1),
            jnp.concatenate([harm_imag, -harm_real], axis=1),
        ],
        axis=0,
    )
    paired_major = paired.transpose(2, 1, 0)
    folded = jnp.einsum(
        "mpj,mjn->mpn", stacked_major, paired_major, preferred_element_type=jnp.float32
    )
    correlation = jnp.einsum(
        "mpk,mr->pkr", folded[:, :, :class_count], rotate_table[0], precision=lax.Precision.HIGHEST
    )
    correlation = correlation + jnp.einsum(
        "mpk,mr->pkr", folded[:, :, class_count:], rotate_table[1], precision=lax.Precision.HIGHEST
    )
    real_wide = harm_real.astype(jnp.float32)
    imag_wide = harm_imag.astype(jnp.float32)
    energy = jnp.sum(real_wide * real_wide + imag_wide * imag_wide, axis=2)
    ref_power = jnp.dot(contrast * contrast, energy.T, precision=lax.Precision.HIGHEST) / angles
    scores = correlation / jnp.sqrt(ref_power + EPSILON)[:, :, None]
    return jnp.max(scores, axis=(1, 2))


def fold_blocks(best_score, ref_piece, per_owner, convert, stacked_major, contrast, rotate_table):
    cycle_count = ref_piece.shape[1]
    row_width = ref_piece.shape[2]
    groups = ref_piece.reshape(-1, per_owner, cycle_count, row_width)

    def per_group(running, class_group):
        return (
            jnp.maximum(
                running, block_scores(stacked_major, contrast, convert(class_group), rotate_table)
            ),
            None,
        )

    best_score, ignored = lax.scan(per_group, best_score, groups)
    return best_score


def on_device(particles, references, class_block, class_local, rotation, shifts, defocus):
    particle_count, cycle_count, row_width = particles.shape
    angles = row_width // 2
    dom_count = lax.axis_size("dom")
    owners = lax.axis_size("cls")
    per_owner = references.shape[0]
    dft_table = angle_table(angles)
    rotate_table = rotation_table(angles, ROT)
    contrast, weighted, unrotated = prepare(particles, rotation, shifts, defocus)
    stacked = jnp.concatenate([weighted[:, :, :angles], weighted[:, :, angles:]], axis=1)
    stacked_major = stacked.transpose(2, 0, 1)
    start_best = jnp.full((particle_count,), -1e30, jnp.float32)

    def transform(samples):
        class_count = samples.shape[0]
        return (
            jnp.dot(
                samples.reshape(class_count * cycle_count, row_width),
                dft_table,
                preferred_element_type=jnp.float32,
            )
            .reshape(class_count, cycle_count, row_width)
            .astype(jnp.bfloat16)
        )

    best_score = fold_blocks(
        start_best,
        lax.all_gather(references, "cls", axis=0, tiled=True),
        per_owner,
        transform,
        stacked_major,
        contrast,
        rotate_table,
    )
    capacity = 2 * particle_count // owners
    cycle_band = cycle_count // dom_count
    owner_of = class_block[:, 0]
    owner_hits = (owner_of[:, None] == jnp.arange(owners, dtype=jnp.int32)[None, :]).astype(
        jnp.int32
    )
    slot_of = jnp.sum((jnp.cumsum(owner_hits, axis=0) - owner_hits) * owner_hits, axis=1)
    target_slot = owner_of * capacity + slot_of
    dispatch = (
        target_slot[:, None] == jnp.arange(owners * capacity, dtype=jnp.int32)[None, :]
    ).astype(jnp.bfloat16)
    spread = unrotated.reshape(particle_count, dom_count, cycle_band * row_width)
    outbox = jnp.einsum("ps,pdf->dsf", dispatch, spread, preferred_element_type=jnp.float32).astype(
        jnp.bfloat16
    )
    labels = jnp.full((owners, capacity), -1, jnp.int32).at[owner_of, slot_of].set(class_local)
    labels = jnp.broadcast_to(labels[None], (dom_count, owners, capacity))
    received, received_labels = (
        lax.all_to_all(
            outbox.reshape(dom_count * owners, capacity, cycle_band * row_width),
            ("dom", "cls"),
            split_axis=0,
            concat_axis=0,
            tiled=True,
        ),
        lax.all_to_all(
            labels.reshape(dom_count * owners, capacity),
            ("dom", "cls"),
            split_axis=0,
            concat_axis=0,
            tiled=True,
        ),
    )
    flat_labels = received_labels.reshape(-1)
    member = (flat_labels[:, None] == jnp.arange(per_owner, dtype=jnp.int32)[None, :]).astype(
        jnp.bfloat16
    )
    class_sums = jnp.einsum(
        "sk,sf->kf",
        member,
        received.reshape(flat_labels.shape[0], cycle_band * row_width),
        preferred_element_type=jnp.float32,
    )
    member_local = (class_local[:, None] == jnp.arange(per_owner, dtype=jnp.int32)[None, :]).astype(
        jnp.float32
    )
    squares = (contrast * contrast).reshape(particle_count, dom_count, cycle_band)
    weights = jnp.einsum(
        "pc,pk,pdr->dckr",
        owner_hits.astype(jnp.float32),
        member_local,
        squares,
        precision=lax.Precision.HIGHEST,
    )
    weights = lax.psum_scatter(
        weights.reshape(dom_count * owners, per_owner * cycle_band),
        ("dom", "cls"),
        scatter_dimension=0,
        tiled=True,
    )
    class_average = class_sums.reshape(per_owner, cycle_band, row_width) / (
        weights.reshape(per_owner, cycle_band)[:, :, None] + 1.0
    )
    return (best_score, class_average)


def solution(mesh):
    placed = (
        P(("dom", "cls"), None, None),
        P("cls", None, None),
        P(("dom", "cls"), None),
        P(("dom", "cls")),
        P(("dom", "cls")),
        P(("dom", "cls"), None),
        P(("dom", "cls")),
    )
    return jax.shard_map(
        on_device,
        mesh=mesh,
        in_specs=placed,
        out_specs=(P(("dom", "cls")), P("cls", "dom", None)),
        check_vma=False,
    )
```

profile of v0, /device:TPU:0, one launch (start us, length us, event | category | flops | bytes accessed | tf_op | source)
XLA Modules:
  0.0 544.9 jit_solution(1248235948160322214)
XLA Ops:
  11.3 4.5 scatter_fusion
  16.4 7.3 %all-to-all-start = ((s32[32,1,12]{2,1,0:T(1,128)}), s32[32,1,12]{2,1,0:T(1,128)S(1)}, u32[]{:S(2)}, u32[]{:S(2)}) async-start(s32[32,1,12]{2,1,0:T(1,128)} %bitcast.8), calls=%async_computation | async-start | bytes 32768 | tf_op jit(solution)/shard_map/all_to_all | solution.py:206
  28.4 13.0 %fusion.22 = (bf16[48,64,144]{2,1,0:T(8,128)(2,1)S(1)}, bf16[48,64,144]{2,1,0:T(8,128)(2,1)S(1)}) fusion(f32[48,144]{1,0:T(8,128)S(1)} %multiply_add_fusion.1, f32[64]{0:T(128)S(1)} %convert_multiply_fusion.1, bf16[48,64,288]{2,1,0:T(8,128)(2,1)S(1)} %copy-done.1), kind=kLoop, calls=%fused_computation.36 | loop fusion | flops 4866048 | bytes 3566848 | tf_op jit(solution)/shard_map/convert.1
  56.5 6.1 %all-to-all-start.1 = ((bf16[32,12,4608]{2,1,0:T(8,128)(2,1)}), bf16[32,12,4608]{2,1,0:T(8,128)(2,1)}, u32[]{:S(2)}, u32[]{:S(2)}) async-start(bf16[32,12,4608]{2,1,0:T(8,128)(2,1)} %reshape.289), calls=%async_computation.1 | async-start | bytes 9437184 | tf_op jit(solution)/shard_map/all_to_all | solution.py:199
  64.8 201.9 %all-reduce = f32[32,400]{1,0:T(8,128)S(1)} all-reduce(f32[32,400]{1,0:T(8,128)S(1)} %reshape.292), channel_id=2, replica_groups=mesh['dom'=4,'cls'=8] {'dom','cls'}, use_global_device_ids=true, to_apply=%region_7.8.clone | all-reduce | flops 12800 | bytes 102400
  275.3 4.1 reshape.290
  287.7 250.4 %while.13 = (s32[]{:T(128)}, f32[48]{0:T(128)}, bf16[8,25,64,288]{3,2,1,0:T(8,128)(2,1)}, bf16[288,288]{1,0:T(8,128)(2,1)}, bf16[144,48,128]{2,1,0:T(8,128)(2,1)...) while((s32[]{:T(128)}, f32[48]{0:T(128)}, ...), condition=%wide.region_3.4_spmd.clone, body=%wide.region_0.3_spmd.clone.sunk | while | flops 513692064 | bytes 26293744 | solution.py:143
  292.8 4.1 copy.46
  303.2 4.2 copy.47
  323.6 4.1 copy.46
  334.0 4.2 copy.47
  338.1 4.1 fusion.125
  354.9 4.1 copy.46
  365.3 4.2 copy.47
  386.3 4.1 copy.46
  396.7 4.2 copy.47
  417.7 4.1 copy.46
  428.1 4.2 copy.47
  449.1 4.1 copy.46
  459.5 4.2 copy.47
  480.5 4.1 copy.46
  490.8 4.2 copy.47
  511.8 4.1 copy.46
  522.2 4.2 copy.47
  (160 shorter events, 223.1 us)
Async XLA Ops:
  7.2 21.2 %copy-start.1 = (bf16[48,64,288]{2,1,0:T(8,128)(2,1)S(1)}, bf16[48,64,288]{2,1,0:T(8,128)(2,1)}, u32[]{:S(2)}) copy-start(bf16[48,64,288]{2,1,0:T(8,128)(2,1)} %param.9) | copy-start | bytes 5308420
  7.2 280.5 %all-gather.2.cloned.1.call-start = ((), (), s32[]{:S(2)}) async-start(), calls=%async_computation.2 | async-start | bytes 11059200 | tf_op jit(solution)/shard_map/all_gather | solution.py:174
  16.4 40.1 %all-to-all-start = ((s32[32,1,12]{2,1,0:T(1,128)}), s32[32,1,12]{2,1,0:T(1,128)S(1)}, u32[]{:S(2)}, u32[]{:S(2)}) async-start(s32[32,1,12]{2,1,0:T(1,128)} %bitcast.8), calls=%async_computation | async-start | bytes 32768 | tf_op jit(solution)/shard_map/all_to_all | solution.py:206
  24.4 17.0 %copy-start.2 = (bf16[144,144]{1,0:T(8,128)(2,1)}, bf16[144,144]{1,0:T(8,128)(2,1)S(1)}, u32[]{:S(2)}) copy-start(bf16[144,144]{1,0:T(8,128)(2,1)S(1)} %fusion.36) | copy-start | bytes 124420
  25.0 16.4 %copy-start.4 = (bf16[144,144]{1,0:T(8,128)(2,1)}, bf16[144,144]{1,0:T(8,128)(2,1)S(1)}, u32[]{:S(2)}) copy-start(bf16[144,144]{1,0:T(8,128)(2,1)S(1)} %get-tuple-element.176) | copy-start | bytes 124420
  25.0 16.4 %copy-start.6 = (bf16[144,144]{1,0:T(8,128)(2,1)}, bf16[144,144]{1,0:T(8,128)(2,1)S(1)}, u32[]{:S(2)}) copy-start(bf16[144,144]{1,0:T(8,128)(2,1)S(1)} %get-tuple-element.177) | copy-start | bytes 124420
  56.4 7.0 %copy-start.8 = (f32[48,8]{1,0:T(8,128)S(1)}, f32[48,8]{1,0:T(8,128)}, u32[]{:S(2)}) copy-start(f32[48,8]{1,0:T(8,128)} %get-tuple-element.168) | copy-start | bytes 4612
  56.4 7.0 %copy-start.10 = (s32[48]{0:T(128)S(1)}, s32[48]{0:T(128)}, u32[]{:S(2)}) copy-start(s32[48]{0:T(128)} %param.12) | copy-start | bytes 580
  56.4 211.0 %copy-start = (bf16[48,64,288]{2,1,0:T(8,128)(2,1)S(1)}, bf16[48,64,288]{2,1,0:T(8,128)(2,1)}, u32[]{:S(2)}) copy-start(bf16[48,64,288]{2,1,0:T(8,128)(2,1)} %get-tuple-element.163) | copy-start | bytes 5308420
  56.5 218.8 %all-to-all-start.1 = ((bf16[32,12,4608]{2,1,0:T(8,128)(2,1)}), bf16[32,12,4608]{2,1,0:T(8,128)(2,1)}, u32[]{:S(2)}, u32[]{:S(2)}) async-start(bf16[32,12,4608]{2,1,0:T(8,128)(2,1)} %reshape.289), calls=%async_computation.1 | async-start | bytes 9437184 | tf_op jit(solution)/shard_map/all_to_all | solution.py:199
  269.1 4.0 copy-start.3
  269.1 4.0 copy-start.5
  269.1 4.0 copy-start.7
  279.4 3.7 copy-start.9
Sparse Core Ops, SparseCore 0:
  10.2 227.3 all-gather.1
where the time goes:
time: 547 us; the launch traced here: 545 us
  blocking collectives  202 us (37%)
  local copies, waits for them, and re-layouts  141 us (26%)
  matrix products  121 us (22%)
  other arithmetic  51.8 us (9%)
  between operations  14.3 us (3%)
  starting transfers between devices  13.5 us (2%)
    unnamed x1, blocking collectives  202 us
    slice x16, local copies, waits for them, and re-layouts, block_scores(): folded[:, :, class_count:]  47.7 us
    slice x8, local copies, waits for them, and re-layouts, block_scores(): folded[:, :, :class_count]  33.4 us
    transpose x8, local copies, waits for them, and re-layouts, block_scores(): paired_major = paired.transpose(2, 1, 0)  32.7 us
    dot_general x8, matrix products, block_scores(): jnp.einsum('mpk,mr->pkr', folded[:, :, :class_count], rotate_table[0], pr...  32.4 us
    dot_general x8, matrix products, block_scores(): jnp.einsum('mpk,mr->pkr', folded[:, :, class_count:], rotate_table[1], pr...  27.4 us
    dot_general x8, matrix products, block_scores(): jnp.einsum('mpj,mjn->mpn', stacked_major, paired_major, preferred_element...  26.3 us
    dot_general x8, matrix products, transform(): jnp.dot(samples.reshape(class_count * cycle_count, row_width), dft_table,...  17.5 us
  transfers between devices with their start and end apart: 3, of which 0 were waited for; matrix products, arithmetic and copies ran while one was open for 12% of the time, Pallas kernels for 0%

commit v1 on v0

v1 whole, which is shorter than its diff:
```python
import functools
import math

import jax
import jax.numpy as jnp
from jax import lax
from jax.experimental import pallas as pl
from jax.experimental.pallas import tpu as pltpu
from jax.sharding import PartitionSpec as P

ROT = 36
BOX = 128
NBINS = 16


EPSILON = 1e-06


def angle_table(angles):
    sample_index = jnp.arange(angles, dtype=jnp.int32)
    turn_count = sample_index[:, None] * sample_index[None, :] % angles
    angle_value = turn_count.astype(jnp.float32) * (2.0 * math.pi / angles)
    cosine = jnp.cos(angle_value)
    sine_part = jnp.sin(angle_value)
    upper_half = jnp.concatenate([cosine, -sine_part], axis=1)
    lower_half = jnp.concatenate([sine_part, cosine], axis=1)
    return jnp.concatenate([upper_half, lower_half], axis=0).astype(jnp.bfloat16)


def ctf_table(bins, cycle_count):
    radius = (jnp.arange(cycle_count, dtype=jnp.int32) + 1).astype(jnp.float32) / cycle_count
    defocus_level = jnp.arange(bins, dtype=jnp.int32).astype(jnp.float32) / bins
    phase = math.pi * (3.0 + 9.0 * defocus_level[:, None]) * (radius[None, :] * radius[None, :])
    return 0.995 * jnp.sin(phase) + 0.1 * jnp.cos(phase)


def ctf_rows(defocus, bins, cycle_count):
    defocus_hits = (defocus[:, None] == jnp.arange(bins, dtype=jnp.int32)[None, :]).astype(
        jnp.float32
    )
    return jnp.dot(defocus_hits, ctf_table(bins, cycle_count), precision=lax.Precision.HIGHEST)


def phase_turns(shifts, cycle_count, angles):
    inner = 8
    outer = cycle_count // inner
    angle_value = jnp.arange(angles, dtype=jnp.int32).astype(jnp.float32) * (2.0 * math.pi / angles)
    along = (
        shifts[:, 0].astype(jnp.float32)[:, None] * jnp.cos(angle_value)[None, :]
        + shifts[:, 1].astype(jnp.float32)[:, None] * jnp.sin(angle_value)[None, :]
    ) * (2.0 * math.pi / BOX)
    fine = jnp.arange(inner, dtype=jnp.int32).astype(jnp.float32)[None, :, None] * along[:, None, :]
    coarse = (jnp.arange(outer, dtype=jnp.int32) * inner).astype(jnp.float32)[
        None, :, None
    ] * along[:, None, :]
    cf, sf = jnp.cos(fine)[:, None], jnp.sin(fine)[:, None]
    cc, sc = jnp.cos(coarse)[:, :, None], jnp.sin(coarse)[:, :, None]
    shape = (shifts.shape[0], cycle_count, angles)
    return (cf * cc - sf * sc).reshape(shape), (sf * cc + cf * sc).reshape(shape)


def prepare(particles, rotation, shifts, defocus):
    particle_count, cycle_count, row_width = particles.shape
    angles = row_width // 2
    cos_phase, sin_phase = phase_turns(shifts, cycle_count, angles)
    real_part = particles[:, :, :angles].astype(jnp.float32)
    imag_part = particles[:, :, angles:].astype(jnp.float32)
    shifted = jnp.concatenate(
        [
            real_part * cos_phase - imag_part * sin_phase,
            real_part * sin_phase + imag_part * cos_phase,
        ],
        axis=2,
    ).astype(jnp.bfloat16)
    spectrum = jnp.dot(
        shifted.reshape(particle_count * cycle_count, row_width),
        angle_table(angles),
        preferred_element_type=jnp.float32,
    ).reshape(particle_count, cycle_count, row_width)
    contrast = ctf_rows(defocus, NBINS, cycle_count)
    weighted = (contrast[:, :, None] * spectrum).astype(jnp.bfloat16)
    rotate_step = angles // ROT
    harmonic = jnp.arange(angles, dtype=jnp.int32)
    turn_count = harmonic[None, :] * (rotate_step * rotation[:, None]) % angles
    angle_value = turn_count.astype(jnp.float32) * (2.0 * math.pi / angles)
    cos_rot = jnp.cos(angle_value)[:, None, :]
    sin_rot = jnp.sin(angle_value)[:, None, :]
    spec_real = spectrum[:, :, :angles]
    spec_imag = spectrum[:, :, angles:]
    turned = jnp.concatenate(
        [spec_real * cos_rot - spec_imag * sin_rot, spec_real * sin_rot + spec_imag * cos_rot],
        axis=2,
    )
    unrotated = (contrast[:, :, None] * turned).astype(jnp.bfloat16)
    return (contrast, weighted, unrotated)


def rotation_major(rows, copies):
    count, cycles, width = rows.shape
    wide = rows.reshape(count, cycles, 2, copies, width // 2 // copies)
    return wide.transpose(4, 0, 2, 3, 1).reshape(width // 2 // copies, count, 2 * copies * cycles)


def remote(src, dst, send, recv, d, c):
    return pltpu.make_async_remote_copy(
        src_ref=src,
        dst_ref=dst,
        send_sem=send,
        recv_sem=recv,
        device_id=(d, c),
        device_id_type=pl.DeviceIdType.MESH,
    )


def spread_kernel(
    doms, owners, fine, h, e, u, lab, hg, eg, ug, lg,
    s1, r1, s2, r2, s3, r3, se, re, su, ru, sl, rl, own,
):
    d = lax.axis_index("dom")
    c = lax.axis_index("cls")
    quarter = h.shape[0] // 4
    inner = d % 4
    base = d - inner
    side = inner % 2
    row = inner // 2
    piece = (side * 2 + row) * quarter
    across = base + (1 - row) * 2 + side
    mate = base + row * 2 + (1 - side)
    plane = doms * fine
    slab = d * fine + c % fine
    first = c - c % fine
    barrier = pltpu.get_barrier_semaphore()
    for i in range(1, owners):
        pl.semaphore_signal(
            barrier, inc=1, device_id=(d, (c + i) % owners), device_id_type=pl.DeviceIdType.MESH
        )
    for i in range(1, plane):
        other = (slab + i) % plane
        pl.semaphore_signal(
            barrier,
            inc=1,
            device_id=(other // fine, first + other % fine),
            device_id_type=pl.DeviceIdType.MESH,
        )
    pl.semaphore_wait(barrier, owners - 1 + plane - 1)
    local = [
        pltpu.make_async_copy(h, hg.at[c], own.at[0]),
        pltpu.make_async_copy(e, eg.at[c], own.at[1]),
        pltpu.make_async_copy(u.at[slab], ug.at[slab], own.at[2]),
        pltpu.make_async_copy(lab, lg.at[slab], own.at[3]),
    ]
    ended = []
    for i in range(1, owners):
        to = (c + i) % owners
        copy = remote(
            h.at[pl.ds(piece, quarter)],
            hg.at[c, pl.ds(piece, quarter)],
            s1.at[i],
            r1.at[i],
            d,
            to,
        )
        copy.start()
        ended.append(copy)
    for i in range(1, owners):
        copy = remote(e, eg.at[c], se.at[i], re.at[i], d, (c + i) % owners)
        copy.start()
        ended.append((copy, remote(e, eg.at[(c + owners - i) % owners], se.at[i], re.at[i], d, c)))
    for i in range(1, plane):
        other = (slab + i) % plane
        source = (slab + plane - i) % plane
        to = (other // fine, first + other % fine)
        copy = remote(u.at[other], ug.at[slab], su.at[i], ru.at[i], *to)
        copy.start()
        ended.append((copy, remote(u.at[other], ug.at[source], su.at[i], ru.at[i], *to)))
        copy = remote(lab, lg.at[slab], sl.at[i], rl.at[i], *to)
        copy.start()
        ended.append((copy, remote(lab, lg.at[source], sl.at[i], rl.at[i], *to)))
    for copy in local:
        copy.start()
    half = 2 * quarter
    other_piece = (side * 2 + 1 - row) * quarter

    def to_mate(i):
        source = (c + owners - i) % owners
        arrived = hg.at[source, pl.ds(other_piece, quarter)]
        remote(arrived, arrived, s2.at[i], r2.at[i], across, c).wait_recv()
        part = hg.at[source, pl.ds(side * half, half)]
        copy = remote(part, part, s3.at[i], r3.at[i], mate, c)
        copy.start()
        taken = hg.at[source, pl.ds((1 - side) * half, half)]
        ended.append((copy, remote(taken, taken, s3.at[i], r3.at[i], mate, c)))

    for i in range(1, owners):
        source = (c + owners - i) % owners
        part = hg.at[source, pl.ds(piece, quarter)]
        remote(part, part, s1.at[i], r1.at[i], d, source).wait_recv()
        copy = remote(part, part, s2.at[i], r2.at[i], across, c)
        copy.start()
        ended.append(copy)
        if i > 1:
            to_mate(i - 1)
    to_mate(owners - 1)
    for copy in ended:
        if isinstance(copy, tuple):
            copy[0].wait_send()
            copy[1].wait_recv()
        else:
            copy.wait_send()
    for copy in local:
        copy.wait()


def spread(h, e, u, lab, doms, owners, fine):
    plane = doms * fine
    dma = pltpu.SemaphoreType.DMA
    anywhere = pl.BlockSpec(memory_space=pl.ANY)
    return pl.pallas_call(
        functools.partial(spread_kernel, doms, owners, fine),
        out_shape=(
            jax.ShapeDtypeStruct((owners,) + h.shape, h.dtype),
            jax.ShapeDtypeStruct((owners,) + e.shape, e.dtype),
            jax.ShapeDtypeStruct(u.shape, u.dtype),
            jax.ShapeDtypeStruct((plane,) + lab.shape, lab.dtype),
        ),
        in_specs=[anywhere] * 4,
        out_specs=(anywhere,) * 4,
        scratch_shapes=[dma((owners,))] * 8 + [dma((plane,))] * 4 + [dma((4,))],
        compiler_params=pltpu.CompilerParams(collective_id=0, has_side_effects=True),
    )(h, e, u, lab)


def owner_kernel(owners, sums, den, sums_out, den_out, s1, r1, s2, r2, own):
    d = lax.axis_index("dom")
    c = lax.axis_index("cls")
    barrier = pltpu.get_barrier_semaphore()
    for i in range(1, owners):
        pl.semaphore_signal(
            barrier, inc=1, device_id=(d, (c + i) % owners), device_id_type=pl.DeviceIdType.MESH
        )
    pl.semaphore_wait(barrier, owners - 1)
    local = [
        pltpu.make_async_copy(sums.at[c], sums_out.at[c], own.at[0]),
        pltpu.make_async_copy(den.at[c], den_out.at[c], own.at[1]),
    ]
    ended = []
    for i in range(1, owners):
        to = (c + i) % owners
        source = (c + owners - i) % owners
        for src, dst, send, recv in ((sums, sums_out, s1, r1), (den, den_out, s2, r2)):
            copy = remote(src.at[to], dst.at[c], send.at[i], recv.at[i], d, to)
            copy.start()
            ended.append(
                (copy, remote(src.at[to], dst.at[source], send.at[i], recv.at[i], d, to))
            )
    for copy in local:
        copy.start()
    for copy, arrival in ended:
        copy.wait_send()
        arrival.wait_recv()
    for copy in local:
        copy.wait()


def to_owners(sums, den, owners):
    dma = pltpu.SemaphoreType.DMA
    anywhere = pl.BlockSpec(memory_space=pl.ANY)
    return pl.pallas_call(
        functools.partial(owner_kernel, owners),
        out_shape=(
            jax.ShapeDtypeStruct(sums.shape, sums.dtype),
            jax.ShapeDtypeStruct(den.shape, den.dtype),
        ),
        in_specs=[anywhere] * 2,
        out_specs=(anywhere,) * 2,
        scratch_shapes=[dma((owners,))] * 4 + [dma((2,))],
        compiler_params=pltpu.CompilerParams(collective_id=1, has_side_effects=True),
    )(sums, den)


def largest_turn(take):
    columns = [[None] * 9 for _ in range(4)]
    for m2 in range(9):
        real, imag = [], []
        for m1 in range(4):
            x, y = take((9 * m1 + 4 * m2) % 36)
            real.append(x)
            imag.append(y)
        ar, ai = real[0] + real[2], imag[0] + imag[2]
        br, bi = real[0] - real[2], imag[0] - imag[2]
        cr, ci = real[1] + real[3], imag[1] + imag[3]
        dr, di = real[1] - real[3], imag[1] - imag[3]
        columns[0][m2] = (ar + cr, ai + ci)
        columns[1][m2] = (br + di, bi - dr)
        columns[2][m2] = (ar - cr, ai - ci)
        columns[3][m2] = (br - di, bi + dr)
    best = None
    for x in columns:
        even = [x[b][0] + x[9 - b][0] for b in range(1, 5)]
        odd = [x[b][1] - x[9 - b][1] for b in range(1, 5)]
        tops = [x[0][0] + even[0] + even[1] + even[2] + even[3]]
        for s in range(1, 5):
            total = x[0][0]
            turn = None
            for b in range(1, 5):
                step = 2.0 * math.pi * (b * s % 9) / 9
                total = total + even[b - 1] * math.cos(step)
                term = odd[b - 1] * math.sin(step)
                turn = term if turn is None else turn + term
            tops.append(total + jnp.abs(turn))
        for top in tops:
            best = top if best is None else jnp.maximum(best, top)
    return best


def score_kernel(lhs, hg, scale, out, folded, best):
    step = pl.program_id(0)
    owners, group, padded, depth = hg.shape
    rows = lhs.shape[1]
    count = rows // 2
    for g in range(group):
        block = hg[:, g].reshape(owners * padded, depth)
        folded[step * group + g] = lax.dot_general(
            lhs[g], block, (((1,), (1,)), ((), ())), preferred_element_type=jnp.float32
        )

    @pl.when(step == pl.num_programs(0) - 1)
    def _():
        def tile(t, carry):
            at = pl.ds(pl.multiple_of(t * 8, 8), 8)
            after = pl.ds(pl.multiple_of(count + t * 8, 8), 8)
            for lane in range(owners * padded // 128):
                cols = pl.ds(lane * 128, 128)

                def take(m):
                    return folded[m, at, cols], folded[m, after, cols]

                best[at, cols] = largest_turn(take)
            return carry

        lax.fori_loop(0, count // 8, tile, 0)
        power = scale[...]
        scores = jnp.where(power < 0.0, -1e30, best[...] * power)
        out[...] = jnp.broadcast_to(jnp.max(scores, axis=1, keepdims=True), out.shape)


def best_scores(lhs, hg, scale):
    turns, rows, depth = lhs.shape
    owners, _, padded, _ = hg.shape
    group = 4
    width = owners * padded
    return pl.pallas_call(
        score_kernel,
        grid=(turns // group,),
        out_shape=jax.ShapeDtypeStruct((rows // 2, 128), jnp.float32),
        in_specs=[
            pl.BlockSpec((group, rows, depth), lambda i: (i, 0, 0)),
            pl.BlockSpec((owners, group, padded, depth), lambda i: (0, i, 0, 0)),
            pl.BlockSpec((rows // 2, width), lambda i: (0, 0)),
        ],
        out_specs=pl.BlockSpec((rows // 2, 128), lambda i: (0, 0)),
        scratch_shapes=[
            pltpu.VMEM((turns, rows, width), jnp.float32),
            pltpu.VMEM((rows // 2, width), jnp.float32),
        ],
        compiler_params=pltpu.CompilerParams(vmem_limit_bytes=48 * 1024 * 1024),
    )(lhs, hg, scale)[:, 0]


def on_device(particles, references, class_block, class_local, rotation, shifts, defocus):
    particle_count, cycle_count, row_width = particles.shape
    angles = row_width // 2
    copies = angles // ROT
    dom_count = lax.axis_size("dom")
    owners = lax.axis_size("cls")
    per_owner = references.shape[0]
    padded = -(-per_owner // 16) * 16
    fine = 2 if owners % 2 == 0 else 1
    plane = dom_count * fine
    thin = cycle_count // plane
    contrast, weighted, unrotated = prepare(particles, rotation, shifts, defocus)
    turned = rotation_major(weighted, copies)
    half = turned.shape[2] // 2
    lhs = jnp.concatenate(
        [turned, jnp.concatenate([-turned[:, :, half:], turned[:, :, :half]], axis=2)], axis=1
    )
    harmonics = (
        jnp.dot(
            references.reshape(per_owner * cycle_count, row_width),
            angle_table(angles),
            preferred_element_type=jnp.float32,
        )
        .reshape(per_owner, cycle_count, row_width)
        .astype(jnp.bfloat16)
    )
    wide = harmonics.astype(jnp.float32)
    energy = jnp.sum(wide * wide, axis=2)
    energy = jnp.pad(energy, ((0, padded - per_owner), (0, -cycle_count % 128)))
    major = jnp.pad(rotation_major(harmonics, copies), ((0, 0), (0, padded - per_owner), (0, 0)))
    outbox = (
        unrotated.reshape(particle_count, plane, thin * row_width).transpose(1, 0, 2)
    )
    class_ids = class_block[:, 0] * per_owner + class_local
    labels = jnp.pad(jnp.stack([class_ids, defocus]), ((0, 6), (0, -particle_count % 128)))
    all_major, all_energy, inbox, inbox_labels = spread(
        major, energy, outbox, labels, dom_count, owners, fine
    )
    ids = inbox_labels[:, 0, :particle_count].reshape(-1)
    bins = inbox_labels[:, 1, :particle_count].reshape(-1)
    member = jnp.arange(owners * per_owner, dtype=jnp.int32)[:, None] == ids[None, :]
    sums = jnp.dot(
        member.astype(jnp.bfloat16),
        inbox.reshape(plane * particle_count, thin * row_width),
        preferred_element_type=jnp.float32,
    ).astype(jnp.bfloat16)
    slab = lax.axis_index("dom") * fine + lax.axis_index("cls") % fine
    table = ctf_table(NBINS, cycle_count)
    table = lax.dynamic_slice_in_dim(table * table, slab * thin, thin, 1)
    hits = (bins[:, None] == jnp.arange(NBINS, dtype=jnp.int32)[None, :]).astype(jnp.float32)
    squares = jnp.dot(hits, table, precision=lax.Precision.HIGHEST)
    den = jnp.dot(member.astype(jnp.float32), squares, precision=lax.Precision.HIGHEST)
    den = den.reshape(owners, per_owner, thin).transpose(0, 2, 1)
    den = jnp.pad(den, ((0, 0), (0, -thin % 8), (0, -per_owner % 128)))
    all_sums, all_den = to_owners(
        sums.reshape(owners, per_owner, thin * row_width), den, owners
    )
    numerator = jnp.sum(
        all_sums.astype(jnp.float32).reshape(owners // fine, fine, per_owner, thin, row_width),
        axis=0,
    )
    denominator = jnp.sum(
        all_den[:, :thin, :per_owner].reshape(owners // fine, fine, thin, per_owner), axis=0
    ).transpose(0, 2, 1)
    class_average = numerator / (denominator[:, :, :, None] + 1.0)
    class_average = class_average.transpose(1, 0, 2, 3).reshape(
        per_owner, fine * thin, row_width
    )
    power = (
        jnp.dot(
            contrast * contrast,
            all_energy[:, :, :cycle_count].reshape(owners * padded, cycle_count).T,
            precision=lax.Precision.HIGHEST,
        )
        / angles
    )
    used = jnp.arange(owners * padded, dtype=jnp.int32) % padded < per_owner
    scale = jnp.where(used[None, :], 1.0 / (angles * jnp.sqrt(power + EPSILON)), -1.0)
    return (best_scores(lhs, all_major, scale), class_average)


def solution(mesh):
    placed = (
        P(("dom", "cls"), None, None),
        P("cls", None, None),
        P(("dom", "cls"), None),
        P(("dom", "cls")),
        P(("dom", "cls")),
        P(("dom", "cls"), None),
        P(("dom", "cls")),
    )
    return jax.shard_map(
        on_device,
        mesh=mesh,
        in_specs=placed,
        out_specs=(P(("dom", "cls")), P("cls", "dom", None)),
        check_vma=False,
    )
```

time: 547 us -> 194 us (0.35)
  the two profiles are of different devices: /device:TPU:0 before, /device:TPU:11 now
where the time goes in v1:
time: 194 us
  Pallas kernels  127 us (65%)
  local copies, waits for them, and re-layouts  42.7 us (22%)
  other arithmetic  17.1 us (9%)
  matrix products  5.83 us (3%)
    pallas_call x1, Pallas kernels, spread(): pl.pallas_call(functools.partial(spread_kernel, doms, owners, fine), out_...  74.3 us
    pallas_call x1, Pallas kernels, to_owners(): pl.pallas_call(functools.partial(owner_kernel, owners), out_shape=(jax.Sh...  43.1 us
    reshape x3, local copies, waits for them, and re-layouts, rotation_major(): wide.transpose(4, 0, 2, 3, 1)  10.6 us
    pallas_call x1, Pallas kernels, best_scores(): pl.pallas_call(score_kernel, grid=(turns // group,), out_shape=jax.ShapeD...  9.67 us
    transpose x1, local copies, waits for them, and re-layouts, rotation_major(): wide.transpose(4, 0, 2, 3, 1)  6.47 us
    convert_element_type x1, local copies, waits for them, and re-layouts, prepare(): weighted = (contrast[:, :, None] * spectrum).astype(jnp.bfloat16)  6.22 us
    another operation x3, other arithmetic  5.24 us
    convert_element_type x2, local copies, waits for them, and re-layouts, prepare(): unrotated = (contrast[:, :, None] * turned).astype(jnp.bfloat16)  5.1 us

profile of v1, /device:TPU:11, one launch (start us, length us, event | category | flops | bytes accessed | tf_op | source)
XLA Modules:
  0.0 193.7 jit_solution(3888951447861055543)
XLA Ops:
  1.6 2.8 %multiply_cosine_fusion.1 = (f32[48,8,144]{2,1,0:T(8,128)S(1)}, f32[48,8,144]{2,1,0:T(8,128)S(1)}, f32[48,8,144]{2,1,0:T(8,128)S(1)}, f32[48,8,144]{2,1,0:T(8,128)S(1)}) fusion(f32[48,144]{1,0:T(8,128)S(1)} %add_multiply_fusion, f32[8]{0:T(128)S(1)} %get-tuple-element.39, f32[8]{0:T(128)S(1)} %get-tuple-element.38), kind=kLoop, calls=%fused_computation.36 | loop fusion | flops 110592 | bytes 912448 | tf_op jit(solution)/shard_map/cos | solution.py:56
  4.4 4.0 %fusion.2 = (bf16[48,64,144]{2,1,0:T(8,128)(2,1)S(1)}, bf16[48,64,144]{2,1,0:T(8,128)(2,1)S(1)}) fusion(f32[48,8,144]{2,1,0:T(8,128)S(1)} %get-tuple-element.26, f32[48,8,144]{2,1,0:T(8,128)S(1)} %get-tuple-element.23, f32[48,8,144]{2,1,0:T(8,128)S(1)} %get-tuple-element.27, f32[48,8,144]{2,1,0:T(8,128)S(1)} %get-tuple-element.22, bf16[48,64,288]{2,1,0:T(8,128)(2,1)} %param.7), kind=kLoop, calls=%fused_computation.10 | loop fusion | flops 7077888 | bytes 4423680 | tf_op jit(solution)/shard_map/convert.7
  9.6 1.7 fusion.5
  11.7 1.1 multiply_subtract_fusion
  13.1 3.2 %fusion = (bf16[48,64,288]{2,1,0:T(8,128)(2,1)}, bf16[48,64,288]{2,1,0:T(8,128)(2,1)}) fusion(f32[48,64,144]{2,1,0:T(8,128)S(1)} %get-tuple-element.17, f32[48,64,144]{2,1,0:T(8,128)S(1)} %get-tuple-element.16, f32[48,64]{1,0:T(8,128)S(1)} %fusion.36, f32[48,64,288]{2,1,0:T(8,128)S(1)} %fusion.5), kind=kLoop, calls=%fused_computation.1 | loop fusion | flops 4423680 | bytes 10629120 | tf_op jit(solution)/shard_map/convert_element_type | solution.py:94
  16.3 3.6 %convert_element_type.143 = bf16[48,8,2304]{2,1,0:T(8,128)(2,1)S(1)} reshape(bf16[48,64,288]{2,1,0:T(8,128)(2,1)} %get-tuple-element.28) | data formatting | bytes 3538944 | tf_op jit(solution)/shard_map/convert_element_type | solution.py:94
  19.9 1.5 copy.40
  21.4 0.9 multiply_reduce_fusion
  22.3 3.1 %convert_element_type.139 = bf16[25,64,2,4,36]{1,0,4,3,2:T(8,128)(2,1)} reshape(bf16[1600,288]{0,1:T(8,128)(2,1)S(1)} %bitcast.70) | data formatting | bytes 1843200 | tf_op jit(solution)/shard_map/convert_element_type | solution.py:394
  25.4 3.1 %copy.26 = bf16[36,25,2,4,64]{4,3,2,1,0:T(4,128)(2,1)S(1)} copy(bf16[36,25,2,4,64]{4,1,0,3,2:T(8,128)(2,1)} %bitcast.67) | data formatting | bytes 1843200 | tf_op jit(solution)/shard_map/reshape | solution.py:101
  28.6 1.6 reshape.241
  30.2 1.2 pad.16.h
  32.7 74.3 %shard_map.86 = (bf16[8,36,32,512]{3,2,1,0:T(8,128)(2,1)}, f32[8,32,128]{2,1,0:T(8,128)}, bf16[8,48,2304]{2,1,0:T(8,128)(2,1)}, s32[8,8,128]{2,1,0:T(8,128)}) custom-call(bf16[36,32,512]{2,1,0:T(8,128)(2,1)} %pad.16.h, f32[32,128]{1,0:T(8,128)} %pad.17.e, bf16[8,48,2304]{2,1,0:T(8,128)(2,1)} %bitcast.68, s32[8,128]{1,0:T(8,128)} %pad.18.lab), custom_call_target="tpu_custom_call" | custom-call | tf_op jit(solution)/shard_map/pallas_call | solution.py:218
  109.5 2.1 %convolution_convert_fusion = bf16[200,2304]{1,0:T(8,128)(2,1)S(1)} fusion(bf16[384,2304]{1,0:T(8,128)(2,1)} %bitcast.69, s32[384]{0:T(512)S(1)} %eq.56), kind=kOutput, calls=%fused_computation.7 | convolution fusion | flops 354432000 | bytes 2692608 | tf_op jit(solution)/shard_map/dot_general | solution.py:411
  111.6 1.3 reshape.232.sums
  112.9 43.1 %shard_map.88 = (bf16[8,25,2304]{2,1,0:T(8,128)(2,1)}, f32[8,8,128]{2,1,0:T(8,128)}) custom-call(bf16[8,25,2304]{2,1,0:T(8,128)(2,1)} %reshape.232.sums, f32[8,8,128]{2,1,0:T(8,128)} %pad.19.den), custom_call_target="tpu_custom_call" | custom-call | tf_op jit(solution)/shard_map/pallas_call | solution.py:268
  156.0 1.8 copy.24
  157.8 3.1 %reshape.239 = f32[4,2,25,8,288]{4,3,1,0,2:T(8,128)} reshape(f32[8,25,2304]{2,0,1:T(8,128)S(1)} %copy.24) | data formatting | bytes 3686400 | tf_op jit(solution)/shard_map/reshape | solution.py:428
  161.0 2.0 %reduce_sum.33 = f32[2,25,8,288]{3,2,0,1:T(8,128)S(1)} reduce(f32[4,2,25,8,288]{4,3,1,0,2:T(8,128)} %reshape.239, f32[]{:T(128)} %constant.92.clone.1), dimensions={0}, to_apply=%region_1.2 | reduce | flops 345600 | bytes 2304004 | tf_op jit(solution)/shard_map/reduce_sum | solution.py:427
  163.1 1.0 fusion.14
  164.3 6.2 %copy.18 = bf16[48,64,288]{1,0,2:T(8,128)(2,1)} copy(bf16[48,64,288]{2,1,0:T(8,128)(2,1)} %get-tuple-element.29) | data formatting | bytes 3538944 | tf_op jit(solution)/shard_map/convert_element_type | solution.py:81
  170.6 6.5 %copy.19 = bf16[36,48,2,4,64]{4,3,2,1,0:T(4,128)(2,1)} copy(bf16[36,48,2,4,64]{4,1,0,3,2:T(8,128)(2,1)} %bitcast.66) | data formatting | bytes 3538944 | tf_op jit(solution)/shard_map/transpose | solution.py:101
  177.0 5.8 %reshape.227 = bf16[36,48,512]{2,1,0:T(8,128)(2,1)S(1)} reshape(bf16[36,48,2,4,64]{4,3,2,1,0:T(4,128)(2,1)} %copy.19) | data formatting | bytes 3538944 | tf_op jit(solution)/shard_map/reshape | solution.py:101
  183.4 9.7 %shard_map.87 = f32[48,128]{1,0:T(8,128)S(1)} custom-call(bf16[36,96,512]{2,1,0:T(8,128)(2,1)S(1)} %maximum_maximum_fusion.lhs, bf16[8,36,32,512]{3,2,1,0:T(8,128)(2,1)} %get-tuple-element.8.hg, f32[48,256]{1,0:T(8,128)S(1)} %fusion.13.scale), custom_call_target="tpu_custom_call" | custom-call | tf_op jit(solution)/shard_map/pallas_call | solution.py:352
  (49 shorter events, 8.0 us)
Async XLA Ops:
  0.6 20.7 %copy-start = (bf16[25,64,288]{2,1,0:T(8,128)(2,1)S(1)}, bf16[25,64,288]{2,1,0:T(8,128)(2,1)}, u32[]{:S(2)}) copy-start(bf16[25,64,288]{2,1,0:T(8,128)(2,1)} %param.8) | copy-start | bytes 2764804
  9.6 1.7 copy-start.5
  11.6 1.2 copy-start.3
  28.5 3.5 %copy-start.6 = (s32[48]{0:T(128)S(1)}, s32[48]{0:T(128)}, u32[]{:S(2)}) copy-start(s32[48]{0:T(128)} %param.10) | copy-start | bytes 580
  28.6 3.5 %copy-start.7 = (s32[48,1]{0,1:T(1,128)S(1)}, s32[48,1]{0,1:T(1,128)}, u32[]{:S(2)}) copy-start(s32[48,1]{0,1:T(1,128)} %param.9) | copy-start | bytes 580
  157.8 5.1 %copy-start.2 = (f32[8,8,128]{2,1,0:T(8,128)S(1)}, f32[8,8,128]{2,1,0:T(8,128)}, u32[]{:S(2)}) copy-start(f32[8,8,128]{2,1,0:T(8,128)} %get-tuple-element.13) | copy-start | bytes 98308
  161.0 3.1 %copy-start.4 = (f32[8,32,128]{2,1,0:T(8,128)S(1)}, f32[8,32,128]{2,1,0:T(8,128)}, u32[]{:S(2)}) copy-start(f32[8,32,128]{2,1,0:T(8,128)} %get-tuple-element.9) | copy-start | bytes 393220
  183.4 10.3 %copy-start.1 = (bf16[25,64,288]{2,1,0:T(8,128)(2,1)S(1)}, bf16[25,64,288]{2,1,0:T(8,128)(2,1)}, u32[]{:S(2)}) copy-start(bf16[25,64,288]{2,1,0:T(8,128)(2,1)} %param.8) | copy-start | bytes 2764804

commit v2 on v1

--- a/solution.py
+++ b/solution.py
@@ -112,36 +112,46 @@
     )
 
 
-def spread_kernel(
-    doms, owners, fine, h, e, u, lab, hg, eg, ug, lg,
-    s1, r1, s2, r2, s3, r3, se, re, su, ru, sl, rl, own,
-):
+def place(h):
     d = lax.axis_index("dom")
     c = lax.axis_index("cls")
-    quarter = h.shape[0] // 4
     inner = d % 4
     base = d - inner
     side = inner % 2
     row = inner // 2
-    piece = (side * 2 + row) * quarter
     across = base + (1 - row) * 2 + side
     mate = base + row * 2 + (1 - side)
+    return d, c, side, row, across, mate
+
+
+def signal_to(barrier, d, c):
+    pl.semaphore_signal(barrier, inc=1, device_id=(d, c), device_id_type=pl.DeviceIdType.MESH)
+
+
+def finish(ended, local):
+    for sent, arrival in ended:
+        sent.wait_send()
+        arrival.wait_recv()
+    for copy in local:
+        copy.wait()
+
+
+def spread_kernel(
+    doms, owners, fine, h, e, u, lab, hg, eg, ug, lg, s1, r1, se, re, su, ru, sl, rl, own
+):
+    d, c, side, row, across, mate = place(h)
+    quarter = h.shape[0] // 4
+    piece = (side * 2 + row) * quarter
+    lines = owners // fine
     plane = doms * fine
     slab = d * fine + c % fine
     first = c - c % fine
     barrier = pltpu.get_barrier_semaphore()
     for i in range(1, owners):
-        pl.semaphore_signal(
-            barrier, inc=1, device_id=(d, (c + i) % owners), device_id_type=pl.DeviceIdType.MESH
-        )
+        signal_to(barrier, d, (c + i) % owners)
     for i in range(1, plane):
         other = (slab + i) % plane
-        pl.semaphore_signal(
-            barrier,
-            inc=1,
-            device_id=(other // fine, first + other % fine),
-            device_id_type=pl.DeviceIdType.MESH,
-        )
+        signal_to(barrier, other // fine, first + other % fine)
     pl.semaphore_wait(barrier, owners - 1 + plane - 1)
     local = [
         pltpu.make_async_copy(h, hg.at[c], own.at[0]),
@@ -150,65 +160,31 @@
         pltpu.make_async_copy(lab, lg.at[slab], own.at[3]),
     ]
     ended = []
-    for i in range(1, owners):
-        to = (c + i) % owners
-        copy = remote(
-            h.at[pl.ds(piece, quarter)],
-            hg.at[c, pl.ds(piece, quarter)],
-            s1.at[i],
-            r1.at[i],
-            d,
-            to,
-        )
-        copy.start()
-        ended.append(copy)
-    for i in range(1, owners):
-        copy = remote(e, eg.at[c], se.at[i], re.at[i], d, (c + i) % owners)
-        copy.start()
-        ended.append((copy, remote(e, eg.at[(c + owners - i) % owners], se.at[i], re.at[i], d, c)))
+
+    def move(src, dst, at, source, send, recv, to):
+        sent = remote(src, dst.at[at], send, recv, *to)
+        sent.start()
+        ended.append((sent, remote(src, dst.at[source], send, recv, *to)))
+
+    part = pl.ds(piece, quarter)
     for i in range(1, plane):
         other = (slab + i) % plane
         source = (slab + plane - i) % plane
         to = (other // fine, first + other % fine)
-        copy = remote(u.at[other], ug.at[slab], su.at[i], ru.at[i], *to)
-        copy.start()
-        ended.append((copy, remote(u.at[other], ug.at[source], su.at[i], ru.at[i], *to)))
-        copy = remote(lab, lg.at[slab], sl.at[i], rl.at[i], *to)
-        copy.start()
-        ended.append((copy, remote(lab, lg.at[source], sl.at[i], rl.at[i], *to)))
+        move(lab, lg, slab, source, sl.at[i], rl.at[i], to)
+        move(u.at[other], ug, slab, source, su.at[i], ru.at[i], to)
+    for i in range(1, lines):
+        to = (c + i * fine) % owners
+        source = (c + owners - i * fine) % owners
+        sent = remote(h.at[part], hg.at[c, part], s1.at[i], r1.at[i], d, to)
+        sent.start()
+        ended.append((sent, remote(h.at[part], hg.at[source, part], s1.at[i], r1.at[i], d, to)))
+    for i in range(1, owners):
+        to = (c + i) % owners
+        move(e, eg, c, (c + owners - i) % owners, se.at[i], re.at[i], (d, to))
     for copy in local:
         copy.start()
-    half = 2 * quarter
-    other_piece = (side * 2 + 1 - row) * quarter
-
-    def to_mate(i):
-        source = (c + owners - i) % owners
-        arrived = hg.at[source, pl.ds(other_piece, quarter)]
-        remote(arrived, arrived, s2.at[i], r2.at[i], across, c).wait_recv()
-        part = hg.at[source, pl.ds(side * half, half)]
-        copy = remote(part, part, s3.at[i], r3.at[i], mate, c)
-        copy.start()
-        taken = hg.at[source, pl.ds((1 - side) * half, half)]
-        ended.append((copy, remote(taken, taken, s3.at[i], r3.at[i], mate, c)))
-
-    for i in range(1, owners):
-        source = (c + owners - i) % owners
-        part = hg.at[source, pl.ds(piece, quarter)]
-        remote(part, part, s1.at[i], r1.at[i], d, source).wait_recv()
-        copy = remote(part, part, s2.at[i], r2.at[i], across, c)
-        copy.start()
-        ended.append(copy)
-        if i > 1:
-            to_mate(i - 1)
-    to_mate(owners - 1)
-    for copy in ended:
-        if isinstance(copy, tuple):
-            copy[0].wait_send()
-            copy[1].wait_recv()
-        else:
-            copy.wait_send()
-    for copy in local:
-        copy.wait()
+    finish(ended, local)
 
 
 def spread(h, e, u, lab, doms, owners, fine):
@@ -225,57 +201,121 @@
         ),
         in_specs=[anywhere] * 4,
         out_specs=(anywhere,) * 4,
-        scratch_shapes=[dma((owners,))] * 8 + [dma((plane,))] * 4 + [dma((4,))],
+        scratch_shapes=[dma((owners,))] * 4 + [dma((plane,))] * 4 + [dma((4,))],
         compiler_params=pltpu.CompilerParams(collective_id=0, has_side_effects=True),
     )(h, e, u, lab)
 
 
-def owner_kernel(owners, sums, den, sums_out, den_out, s1, r1, s2, r2, own):
-    d = lax.axis_index("dom")
-    c = lax.axis_index("cls")
+def owner_kernel(
+    owners, fine, hg_in, sums, den, hg, sums_out, den_out,
+    sx, rx, sy, ry, sm, rm, s1, r1, s2, r2, own,
+):
+    d, c, side, row, across, mate = place(hg)
+    quarter = hg.shape[1] // 4
+    half = 2 * quarter
+    mine = pl.ds((side * 2 + row) * quarter, quarter)
+    theirs = pl.ds((side * 2 + 1 - row) * quarter, quarter)
+    here = pl.ds(side * half, half)
+    there = pl.ds((1 - side) * half, half)
+    lines = owners // fine
     barrier = pltpu.get_barrier_semaphore()
     for i in range(1, owners):
-        pl.semaphore_signal(
-            barrier, inc=1, device_id=(d, (c + i) % owners), device_id_type=pl.DeviceIdType.MESH
-        )
-    pl.semaphore_wait(barrier, owners - 1)
+        signal_to(barrier, d, (c + i) % owners)
+    signal_to(barrier, across, c)
+    signal_to(barrier, mate, c)
+    pl.semaphore_wait(barrier, owners + 1)
     local = [
         pltpu.make_async_copy(sums.at[c], sums_out.at[c], own.at[0]),
         pltpu.make_async_copy(den.at[c], den_out.at[c], own.at[1]),
     ]
     ended = []
+
+    def shard(col, line):
+        return (c - c % fine + line * fine + (c % fine + col) % fine) % owners
+
+    def send(source, taken, part, other, sems, to):
+        piece = hg.at[source, part]
+        sent = remote(piece, piece, sems[0], sems[1], *to)
+        sent.start()
+        arrival = remote(piece, hg.at[taken, other], sems[0], sems[1], *to)
+        ended.append((sent, arrival))
+        return arrival
+
+    def to_across(source, k):
+        return send(source, source, mine, theirs, (sy.at[k], ry.at[k]), (across, c))
+
+    def to_mate(source, k):
+        send(source, source, here, there, (sm.at[k], rm.at[k]), (mate, c))
+
+    from_side = []
+    for col in range(1, fine):
+        to = (d, c - c % fine + (c % fine + col) % fine)
+        back = (fine - col) % fine
+        for line in range(lines):
+            k = col * lines + line
+            from_side.append(
+                (
+                    shard(back, line),
+                    k,
+                    send(
+                        shard(0, line),
+                        shard(back, line),
+                        mine,
+                        mine,
+                        (sx.at[k], rx.at[k]),
+                        to,
+                    ),
+                )
+            )
+    waiting = []
+    for line in range(1, lines):
+        waiting.append((shard(0, line), line, to_across(shard(0, line), line)))
     for i in range(1, owners):
         to = (c + i) % owners
         source = (c + owners - i) % owners
-        for src, dst, send, recv in ((sums, sums_out, s1, r1), (den, den_out, s2, r2)):
-            copy = remote(src.at[to], dst.at[c], send.at[i], recv.at[i], d, to)
-            copy.start()
-            ended.append(
-                (copy, remote(src.at[to], dst.at[source], send.at[i], recv.at[i], d, to))
-            )
+        for src, dst, out, into in ((sums, sums_out, s1, r1), (den, den_out, s2, r2)):
+            sent = remote(src.at[to], dst.at[c], out.at[i], into.at[i], d, to)
+            sent.start()
+            ended.append((sent, remote(src.at[to], dst.at[source], out.at[i], into.at[i], d, to)))
     for copy in local:
         copy.start()
-    for copy, arrival in ended:
-        copy.wait_send()
+    seen = set()
+    for source, k, arrival in from_side:
         arrival.wait_recv()
+        seen.add(id(arrival))
+        waiting.append((source, k, to_across(source, k)))
+        ready = waiting.pop(0)
+        ready[2].wait_recv()
+        seen.add(id(ready[2]))
+        to_mate(ready[0], ready[1])
+    for source, k, arrival in waiting:
+        arrival.wait_recv()
+        seen.add(id(arrival))
+        to_mate(source, k)
+    for sent, arrival in ended:
+        sent.wait_send()
+        if id(arrival) not in seen:
+            arrival.wait_recv()
     for copy in local:
         copy.wait()
 
 
-def to_owners(sums, den, owners):
+def to_owners(hg, sums, den, owners, fine):
     dma = pltpu.SemaphoreType.DMA
     anywhere = pl.BlockSpec(memory_space=pl.ANY)
     return pl.pallas_call(
-        functools.partial(owner_kernel, owners),
+        functools.partial(owner_kernel, owners, fine),
         out_shape=(
+            jax.ShapeDtypeStruct(hg.shape, hg.dtype),
             jax.ShapeDtypeStruct(sums.shape, sums.dtype),
             jax.ShapeDtypeStruct(den.shape, den.dtype),
         ),
-        in_specs=[anywhere] * 2,
-        out_specs=(anywhere,) * 2,
-        scratch_shapes=[dma((owners,))] * 4 + [dma((2,))],
+        in_specs=[anywhere] * 3,
+        out_specs=(anywhere,) * 3,
+        input_output_aliases={0: 0},
+        scratch_shapes=[dma((owners,))] * 10 + [dma((2,))],
         compiler_params=pltpu.CompilerParams(collective_id=1, has_side_effects=True),
-    )(sums, den)
+    )(hg, sums, den)
 
 
 def largest_turn(take):
@@ -421,8 +461,8 @@
     den = jnp.dot(member.astype(jnp.float32), squares, precision=lax.Precision.HIGHEST)
     den = den.reshape(owners, per_owner, thin).transpose(0, 2, 1)
     den = jnp.pad(den, ((0, 0), (0, -thin % 8), (0, -per_owner % 128)))
-    all_sums, all_den = to_owners(
-        sums.reshape(owners, per_owner, thin * row_width), den, owners
+    all_major, all_sums, all_den = to_owners(
+        all_major, sums.reshape(owners, per_owner, thin * row_width), den, owners, fine
     )
     numerator = jnp.sum(
         all_sums.astype(jnp.float32).reshape(owners // fine, fine, per_owner, thin, row_width),

time: 194 us -> 178 us (0.918)
  the two profiles are of different devices: /device:TPU:11 before, /device:TPU:0 now
where the time goes in v2:
time: 178 us; the launch traced here: 177 us
  Pallas kernels  111 us (62%)
  local copies, waits for them, and re-layouts  42.7 us (24%)
  other arithmetic  17.1 us (10%)
  matrix products  5.83 us (3%)
    pallas_call x1, Pallas kernels, spread(): pl.pallas_call(functools.partial(spread_kernel, doms, owners, fine), out_...  50.8 us
    pallas_call x1, Pallas kernels, to_owners(): pl.pallas_call(functools.partial(owner_kernel, owners, fine), out_shape=(...  50.2 us
    reshape x3, local copies, waits for them, and re-layouts, rotation_major(): wide.transpose(4, 0, 2, 3, 1)  10.6 us
    pallas_call x1, Pallas kernels, best_scores(): pl.pallas_call(score_kernel, grid=(turns // group,), out_shape=jax.ShapeD...  9.67 us
    transpose x1, local copies, waits for them, and re-layouts, rotation_major(): wide.transpose(4, 0, 2, 3, 1)  6.47 us
    convert_element_type x1, local copies, waits for them, and re-layouts, prepare(): weighted = (contrast[:, :, None] * spectrum).astype(jnp.bfloat16)  6.22 us
    another operation x3, other arithmetic  5.24 us
    convert_element_type x2, local copies, waits for them, and re-layouts, prepare(): unrotated = (contrast[:, :, None] * turned).astype(jnp.bfloat16)  5.1 us

profile of v2, /device:TPU:0, one launch (start us, length us, event | category | flops | bytes accessed | tf_op | source)
XLA Modules:
  0.0 177.3 jit_solution(18198424999979475971)
XLA Ops:
  1.6 2.8 %multiply_cosine_fusion.1 = (f32[48,8,144]{2,1,0:T(8,128)S(1)}, f32[48,8,144]{2,1,0:T(8,128)S(1)}, f32[48,8,144]{2,1,0:T(8,128)S(1)}, f32[48,8,144]{2,1,0:T(8,128)S(1)}) fusion(f32[48,144]{1,0:T(8,128)S(1)} %add_multiply_fusion, f32[8]{0:T(128)S(1)} %get-tuple-element.41, f32[8]{0:T(128)S(1)} %get-tuple-element.40), kind=kLoop, calls=%fused_computation.36 | loop fusion | flops 110592 | bytes 912448 | tf_op jit(solution)/shard_map/cos | solution.py:56
  4.4 4.0 %fusion.2 = (bf16[48,64,144]{2,1,0:T(8,128)(2,1)S(1)}, bf16[48,64,144]{2,1,0:T(8,128)(2,1)S(1)}) fusion(f32[48,8,144]{2,1,0:T(8,128)S(1)} %get-tuple-element.28, f32[48,8,144]{2,1,0:T(8,128)S(1)} %get-tuple-element.25, f32[48,8,144]{2,1,0:T(8,128)S(1)} %get-tuple-element.29, f32[48,8,144]{2,1,0:T(8,128)S(1)} %get-tuple-element.24, bf16[48,64,288]{2,1,0:T(8,128)(2,1)} %param.7), kind=kLoop, calls=%fused_computation.10 | loop fusion | flops 7077888 | bytes 4423680 | tf_op jit(solution)/shard_map/convert.7
  9.6 1.7 fusion.5
  11.7 1.1 multiply_subtract_fusion
  13.1 3.2 %fusion = (bf16[48,64,288]{2,1,0:T(8,128)(2,1)}, bf16[48,64,288]{2,1,0:T(8,128)(2,1)}) fusion(f32[48,64,144]{2,1,0:T(8,128)S(1)} %get-tuple-element.19, f32[48,64,144]{2,1,0:T(8,128)S(1)} %get-tuple-element.18, f32[48,64]{1,0:T(8,128)S(1)} %fusion.36, f32[48,64,288]{2,1,0:T(8,128)S(1)} %fusion.5), kind=kLoop, calls=%fused_computation.1 | loop fusion | flops 4423680 | bytes 10629120 | tf_op jit(solution)/shard_map/convert_element_type | solution.py:94
  16.3 3.6 %convert_element_type.143 = bf16[48,8,2304]{2,1,0:T(8,128)(2,1)S(1)} reshape(bf16[48,64,288]{2,1,0:T(8,128)(2,1)} %get-tuple-element.30) | data formatting | bytes 3538944 | tf_op jit(solution)/shard_map/convert_element_type | solution.py:94
  19.9 1.5 copy.41
  21.4 0.9 multiply_reduce_fusion
  22.3 3.1 %convert_element_type.139 = bf16[25,64,2,4,36]{1,0,4,3,2:T(8,128)(2,1)} reshape(bf16[1600,288]{0,1:T(8,128)(2,1)S(1)} %bitcast.70) | data formatting | bytes 1843200 | tf_op jit(solution)/shard_map/convert_element_type | solution.py:434
  25.4 3.1 %copy.27 = bf16[36,25,2,4,64]{4,3,2,1,0:T(4,128)(2,1)S(1)} copy(bf16[36,25,2,4,64]{4,1,0,3,2:T(8,128)(2,1)} %bitcast.67) | data formatting | bytes 1843200 | tf_op jit(solution)/shard_map/reshape | solution.py:101
  28.6 1.6 reshape.241
  30.2 1.2 pad.16.h
  32.7 50.8 %shard_map.86 = (bf16[8,36,32,512]{3,2,1,0:T(8,128)(2,1)}, f32[8,32,128]{2,1,0:T(8,128)}, bf16[8,48,2304]{2,1,0:T(8,128)(2,1)}, s32[8,8,128]{2,1,0:T(8,128)}) custom-call(bf16[36,32,512]{2,1,0:T(8,128)(2,1)} %pad.16.h, f32[32,128]{1,0:T(8,128)} %pad.17.e, bf16[8,48,2304]{2,1,0:T(8,128)(2,1)} %bitcast.68, s32[8,128]{1,0:T(8,128)} %pad.18.lab), custom_call_target="tpu_custom_call" | custom-call | tf_op jit(solution)/shard_map/pallas_call | solution.py:194
  86.0 2.1 %convolution_convert_fusion = bf16[200,2304]{1,0:T(8,128)(2,1)S(1)} fusion(bf16[384,2304]{1,0:T(8,128)(2,1)} %bitcast.69, s32[384]{0:T(512)S(1)} %eq.56), kind=kOutput, calls=%fused_computation.7 | convolution fusion | flops 354432000 | bytes 2692608 | tf_op jit(solution)/shard_map/dot_general | solution.py:451
  88.1 1.3 reshape.231.sums
  89.4 50.2 %shard_map.87 = (bf16[8,36,32,512]{3,2,1,0:T(8,128)(2,1)}, bf16[8,25,2304]{2,1,0:T(8,128)(2,1)}, f32[8,8,128]{2,1,0:T(8,128)}) custom-call(bf16[8,36,32,512]{3,2,1,0:T(8,128)(2,1)} %get-tuple-element.9.hg_in, bf16[8,25,2304]{2,1,0:T(8,128)(2,1)} %reshape.231.sums, f32[8,8,128]{2,1,0:T(8,128)} %pad.19.den), custom_call_target="tpu_custom_call", output_to_operand_aliasing={{0}: (0, {})} | custom-call | tf_op jit(solution)/shard_map/pallas_call | solution.py:306
  139.6 1.8 %copy.25 = f32[8,25,2304]{2,0,1:T(8,128)S(1)} copy(bf16[8,25,2304]{2,1,0:T(8,128)(2,1)} %get-tuple-element.14) | data formatting | bytes 2764800 | tf_op jit(solution)/shard_map/reshape | solution.py:468
  141.4 3.1 %reshape.239 = f32[4,2,25,8,288]{4,3,1,0,2:T(8,128)} reshape(f32[8,25,2304]{2,0,1:T(8,128)S(1)} %copy.25) | data formatting | bytes 3686400 | tf_op jit(solution)/shard_map/reshape | solution.py:468
  144.6 2.0 %reduce_sum.33 = f32[2,25,8,288]{3,2,0,1:T(8,128)S(1)} reduce(f32[4,2,25,8,288]{4,3,1,0,2:T(8,128)} %reshape.239, f32[]{:T(128)} %constant.92.clone.1), dimensions={0}, to_apply=%region_1.2 | reduce | flops 345600 | bytes 2304004 | tf_op jit(solution)/shard_map/reduce_sum | solution.py:467
  146.7 1.0 fusion.14
  147.9 6.2 %copy.19 = bf16[48,64,288]{1,0,2:T(8,128)(2,1)} copy(bf16[48,64,288]{2,1,0:T(8,128)(2,1)} %get-tuple-element.31) | data formatting | bytes 3538944 | tf_op jit(solution)/shard_map/convert_element_type | solution.py:81
  154.1 6.5 %copy.20 = bf16[36,48,2,4,64]{4,3,2,1,0:T(4,128)(2,1)} copy(bf16[36,48,2,4,64]{4,1,0,3,2:T(8,128)(2,1)} %bitcast.66) | data formatting | bytes 3538944 | tf_op jit(solution)/shard_map/transpose | solution.py:101
  160.6 5.8 %reshape.227 = bf16[36,48,512]{2,1,0:T(8,128)(2,1)S(1)} reshape(bf16[36,48,2,4,64]{4,3,2,1,0:T(4,128)(2,1)} %copy.20) | data formatting | bytes 3538944 | tf_op jit(solution)/shard_map/reshape | solution.py:101
  167.0 9.7 %shard_map.88 = f32[48,128]{1,0:T(8,128)S(1)} custom-call(bf16[36,96,512]{2,1,0:T(8,128)(2,1)S(1)} %maximum_maximum_fusion.lhs, bf16[8,36,32,512]{3,2,1,0:T(8,128)(2,1)} %get-tuple-element.12.hg, f32[48,256]{1,0:T(8,128)S(1)} %fusion.13.scale), custom_call_target="tpu_custom_call" | custom-call | tf_op jit(solution)/shard_map/pallas_call | solution.py:392
  (49 shorter events, 8.0 us)
Async XLA Ops:
  0.6 20.7 %copy-start = (bf16[25,64,288]{2,1,0:T(8,128)(2,1)S(1)}, bf16[25,64,288]{2,1,0:T(8,128)(2,1)}, u32[]{:S(2)}) copy-start(bf16[25,64,288]{2,1,0:T(8,128)(2,1)} %param.8) | copy-start | bytes 2764804
  9.6 1.7 copy-start.5
  11.6 1.2 copy-start.3
  28.5 3.5 %copy-start.6 = (s32[48]{0:T(128)S(1)}, s32[48]{0:T(128)}, u32[]{:S(2)}) copy-start(s32[48]{0:T(128)} %param.10) | copy-start | bytes 580
  28.6 3.5 %copy-start.7 = (s32[48,1]{0,1:T(1,128)S(1)}, s32[48,1]{0,1:T(1,128)}, u32[]{:S(2)}) copy-start(s32[48,1]{0,1:T(1,128)} %param.9) | copy-start | bytes 580
  141.4 5.1 %copy-start.2 = (f32[8,8,128]{2,1,0:T(8,128)S(1)}, f32[8,8,128]{2,1,0:T(8,128)}, u32[]{:S(2)}) copy-start(f32[8,8,128]{2,1,0:T(8,128)} %get-tuple-element.15) | copy-start | bytes 98308
  144.6 3.1 %copy-start.4 = (f32[8,32,128]{2,1,0:T(8,128)S(1)}, f32[8,32,128]{2,1,0:T(8,128)}, u32[]{:S(2)}) copy-start(f32[8,32,128]{2,1,0:T(8,128)} %get-tuple-element.13) | copy-start | bytes 393220
  167.0 10.3 %copy-start.1 = (bf16[25,64,288]{2,1,0:T(8,128)(2,1)S(1)}, bf16[25,64,288]{2,1,0:T(8,128)(2,1)}, u32[]{:S(2)}) copy-start(bf16[25,64,288]{2,1,0:T(8,128)(2,1)} %param.8) | copy-start | bytes 2764804

commit v3 on v2

--- a/solution.py
+++ b/solution.py
@@ -78,7 +78,6 @@
         preferred_element_type=jnp.float32,
     ).reshape(particle_count, cycle_count, row_width)
     contrast = ctf_rows(defocus, NBINS, cycle_count)
-    weighted = (contrast[:, :, None] * spectrum).astype(jnp.bfloat16)
     rotate_step = angles // ROT
     harmonic = jnp.arange(angles, dtype=jnp.int32)
     turn_count = harmonic[None, :] * (rotate_step * rotation[:, None]) % angles
@@ -92,13 +91,75 @@
         axis=2,
     )
     unrotated = (contrast[:, :, None] * turned).astype(jnp.bfloat16)
-    return (contrast, weighted, unrotated)
-
-
-def rotation_major(rows, copies):
+    return (contrast, shifted, unrotated)
+
+
+def major_kernel(copies, both, rows, gain, table, out, energy, wide):
+    pairs, lanes = gain.shape
+    width = table.shape[0]
+    turns = width // 2 // copies
+    cycles = lanes // 2
+
+    def transform(i, carry):
+        both_rows = jnp.concatenate([rows[i], rows[pairs + i]], axis=0)
+        spectrum = lax.dot_general(
+            table[...],
+            both_rows,
+            (((1,), (1,)), ((), ())),
+            preferred_element_type=jnp.float32,
+        )
+        spectrum = (spectrum * gain[pl.ds(i, 1), :]).astype(jnp.bfloat16).astype(jnp.float32)
+        energy[pl.ds(i, 1), :] = jnp.sum(spectrum * spectrum, axis=0, keepdims=True)
+        wide[pl.ds(i, width, stride=pairs), :] = spectrum
+        return carry
+
+    lax.fori_loop(0, pairs, transform, 0)
+    low = lax.broadcasted_iota(jnp.int32, (pairs, lanes), 1) < cycles
+
+    def gather(m, carry):
+        def part(index):
+            at = (index * turns + m) * pairs
+            return wide[pl.ds(pl.multiple_of(at, 8), pairs), :]
+
+        tops, ends = [], []
+        for index in range(0, 2 * copies, 2):
+            x, y = part(index), part(index + 1)
+            tops.append(jnp.where(low, x, pltpu.roll(y, cycles, 1)))
+            ends.append(jnp.where(low, pltpu.roll(x, cycles, 1), y))
+        half = len(tops) // 2
+        full = jnp.concatenate(
+            [jnp.concatenate(tops, axis=1), jnp.concatenate(ends, axis=1)], axis=0
+        )
+        out[m, pl.ds(0, 2 * pairs), :] = full.astype(out.dtype)
+        if both:
+            tops = [-x for x in tops[half:]] + tops[:half]
+            ends = [-x for x in ends[half:]] + ends[:half]
+            full = jnp.concatenate(
+                [jnp.concatenate(tops, axis=1), jnp.concatenate(ends, axis=1)], axis=0
+            )
+            out[m, pl.ds(2 * pairs, 2 * pairs), :] = full.astype(out.dtype)
+        return carry
+
+    lax.fori_loop(0, turns, gather, 0)
+
+
+def rotation_major(rows, gain, table, copies, both):
     count, cycles, width = rows.shape
-    wide = rows.reshape(count, cycles, 2, copies, width // 2 // copies)
-    return wide.transpose(4, 0, 2, 3, 1).reshape(width // 2 // copies, count, 2 * copies * cycles)
+    pairs = count // 2
+    turns = width // 2 // copies
+    paired = jnp.concatenate([gain[:pairs], gain[pairs:]], axis=1)
+    out, energy = pl.pallas_call(
+        functools.partial(major_kernel, copies, both),
+        out_shape=(
+            jax.ShapeDtypeStruct((turns, count * (2 if both else 1), 2 * copies * cycles), rows.dtype),
+            jax.ShapeDtypeStruct((pairs, 2 * cycles), jnp.float32),
+        ),
+        in_specs=[pl.BlockSpec(memory_space=pltpu.VMEM)] * 3,
+        out_specs=(pl.BlockSpec(memory_space=pltpu.VMEM),) * 2,
+        scratch_shapes=[pltpu.VMEM((width * pairs, 2 * cycles), jnp.float32)],
+        compiler_params=pltpu.CompilerParams(vmem_limit_bytes=32 * 1024 * 1024),
+    )(rows, paired, table)
+    return out, jnp.concatenate([energy[:, :cycles], energy[:, cycles:]], axis=0)
 
 
 def remote(src, dst, send, recv, d, c):
@@ -199,7 +260,7 @@
             jax.ShapeDtypeStruct(u.shape, u.dtype),
             jax.ShapeDtypeStruct((plane,) + lab.shape, lab.dtype),
         ),
-        in_specs=[anywhere] * 4,
+        in_specs=[pl.BlockSpec(memory_space=pltpu.VMEM)] * 4,
         out_specs=(anywhere,) * 4,
         scratch_shapes=[dma((owners,))] * 4 + [dma((plane,))] * 4 + [dma((4,))],
         compiler_params=pltpu.CompilerParams(collective_id=0, has_side_effects=True),
@@ -310,7 +371,7 @@
             jax.ShapeDtypeStruct(sums.shape, sums.dtype),
             jax.ShapeDtypeStruct(den.shape, den.dtype),
         ),
-        in_specs=[anywhere] * 3,
+        in_specs=[anywhere] + [pl.BlockSpec(memory_space=pltpu.VMEM)] * 2,
         out_specs=(anywhere,) * 3,
         input_output_aliases={0: 0},
         scratch_shapes=[dma((owners,))] * 10 + [dma((2,))],
@@ -418,25 +479,17 @@
     fine = 2 if owners % 2 == 0 else 1
     plane = dom_count * fine
     thin = cycle_count // plane
-    contrast, weighted, unrotated = prepare(particles, rotation, shifts, defocus)
-    turned = rotation_major(weighted, copies)
-    half = turned.shape[2] // 2
-    lhs = jnp.concatenate(
-        [turned, jnp.concatenate([-turned[:, :, half:], turned[:, :, :half]], axis=2)], axis=1
-    )
-    harmonics = (
-        jnp.dot(
-            references.reshape(per_owner * cycle_count, row_width),
-            angle_table(angles),
-            preferred_element_type=jnp.float32,
-        )
-        .reshape(per_owner, cycle_count, row_width)
-        .astype(jnp.bfloat16)
-    )
-    wide = harmonics.astype(jnp.float32)
-    energy = jnp.sum(wide * wide, axis=2)
-    energy = jnp.pad(energy, ((0, padded - per_owner), (0, -cycle_count % 128)))
-    major = jnp.pad(rotation_major(harmonics, copies), ((0, 0), (0, padded - per_owner), (0, 0)))
+    contrast, shifted, unrotated = prepare(particles, rotation, shifts, defocus)
+    table = angle_table(angles).T
+    lhs, _ = rotation_major(shifted, contrast, table, copies, True)
+    major, energy = rotation_major(
+        jnp.pad(references, ((0, padded - per_owner), (0, 0), (0, 0))),
+        jnp.ones((padded, cycle_count), jnp.float32),
+        table,
+        copies,
+        False,
+    )
+    energy = jnp.pad(energy, ((0, 0), (0, -cycle_count % 128)))
     outbox = (
         unrotated.reshape(particle_count, plane, thin * row_width).transpose(1, 0, 2)
     )

time: 178 us -> 161 us (0.904)
  local copies, waits for them, and re-layouts: 42.7 us -> 20.5 us
  Pallas kernels: 111 us -> 117 us
    pallas_call x0 -> x2, Pallas kernels: none -> 17 us  [rotation_major(): pl.pallas_call(functools.partial(major_kernel, copies, both), out_shape=(...]
    pallas_call x1, Pallas kernels: 50.8 us -> 37.7 us  [spread(): pl.pallas_call(functools.partial(spread_kernel, doms, owners, fine), out_...]
    reshape x3 -> x0, local copies, waits for them, and re-layouts: 10.6 us -> none  [rotation_major(): wide.transpose(4, 0, 2, 3, 1)]
    convert_element_type x2 -> x0, local copies, waits for them, and re-layouts: 9.35 us -> none  [the longest x1 6.22 us: prepare(): weighted = (contrast[:, :, None] * spectrum).astype(jnp.bfloat16)]
    transpose x1 -> x0, local copies, waits for them, and re-layouts: 6.47 us -> none  [rotation_major(): wide.transpose(4, 0, 2, 3, 1)]
    convert_element_type x2, local copies, waits for them, and re-layouts: 5.1 us -> 7.59 us  [prepare(): unrotated = (contrast[:, :, None] * turned).astype(jnp.bfloat16)]
    pallas_call x1, Pallas kernels: 50.2 us -> 52.5 us  [to_owners(): pl.pallas_call(functools.partial(owner_kernel, owners, fine), out_shape=(...]
    reshape x2, local copies, waits for them, and re-layouts: 4.95 us -> 7.15 us  [on_device(): all_sums.astype(jnp.float32)]
where the time goes in v3:
time: 161 us
  Pallas kernels  117 us (73%)
  local copies, waits for them, and re-layouts  20.5 us (13%)
  other arithmetic  17.7 us (11%)
  matrix products  4.91 us (3%)
    pallas_call x1, Pallas kernels, to_owners(): pl.pallas_call(functools.partial(owner_kernel, owners, fine), out_shape=(...  52.5 us
    pallas_call x1, Pallas kernels, spread(): pl.pallas_call(functools.partial(spread_kernel, doms, owners, fine), out_...  37.7 us
    pallas_call x2, Pallas kernels, rotation_major(): pl.pallas_call(functools.partial(major_kernel, copies, both), out_shape=(...  17 us
    pallas_call x1, Pallas kernels, best_scores(): pl.pallas_call(score_kernel, grid=(turns // group,), out_shape=jax.ShapeD...  9.57 us
    convert_element_type x2, local copies, waits for them, and re-layouts, prepare(): unrotated = (contrast[:, :, None] * turned).astype(jnp.bfloat16)  7.59 us
    reshape x2, local copies, waits for them, and re-layouts, on_device(): all_sums.astype(jnp.float32)  7.15 us
    another operation x3, other arithmetic  4.9 us

profile of v3, /device:TPU:0, one launch (start us, length us, event | category | flops | bytes accessed | tf_op | source)
XLA Modules:
  0.0 160.8 jit_solution(2590806298800692433)
XLA Ops:
  0.7 0.8 convert_bitcast_fusion.1
  1.5 2.8 %multiply_cosine_fusion.1 = (f32[48,8,144]{2,1,0:T(8,128)S(1)}, f32[48,8,144]{2,1,0:T(8,128)S(1)}, f32[48,8,144]{2,1,0:T(8,128)S(1)}, f32[48,8,144]{2,1,0:T(8,128)S(1)}) fusion(f32[48,144]{1,0:T(8,128)S(1)} %add_multiply_fusion, f32[8]{0:T(128)S(1)} %get-tuple-element.45, f32[8]{0:T(128)S(1)} %get-tuple-element.44), kind=kLoop, calls=%fused_computation.28 | loop fusion | flops 110592 | bytes 912448 | tf_op jit(solution)/shard_map/cos | solution.py:56
  4.3 3.7 %fusion.2 = (bf16[48,64,144]{2,1,0:T(8,128)(2,1)S(1)}, bf16[48,64,144]{2,1,0:T(8,128)(2,1)S(1)}) fusion(f32[48,8,144]{2,1,0:T(8,128)S(1)} %get-tuple-element.32, f32[48,8,144]{2,1,0:T(8,128)S(1)} %get-tuple-element.29, f32[48,8,144]{2,1,0:T(8,128)S(1)} %get-tuple-element.33, f32[48,8,144]{2,1,0:T(8,128)S(1)} %get-tuple-element.28, bf16[48,64,288]{2,1,0:T(8,128)(2,1)} %param.7), kind=kLoop, calls=%fused_computation.8 | loop fusion | flops 7077888 | bytes 4423680 | tf_op jit(solution)/shard_map/convert.7
  8.0 0.9 pad_maximum_fusion.rows
  9.0 0.6 negate_convert_fusion
  10.2 1.7 %fusion.12 = f32[48,64,288]{2,1,0:T(8,128)S(1)} fusion(bf16[48,64,288]{2,1,0:T(8,128)(2,1)S(1)} %pad_maximum_fusion.rows, bf16[144,144]{0,1:T(8,128)(2,1)S(1)} %get-tuple-element.47, bf16[144,144]{0,1:T(8,128)(2,1)S(1)} %fusion.22, bf16[144,144]{0,1:T(8,128)(2,1)S(1)} %get-tuple-element.46), kind=kOutput, calls=%fused_computation.32 | convolution fusion | flops 510271488 | bytes 5432832 | tf_op jit(solution)/shard_map/dot_general | solution.py:75
  12.2 1.2 multiply_subtract_fusion
  13.7 2.8 %fusion = bf16[48,64,288]{2,1,0:T(8,128)(2,1)} fusion(f32[48,64,144]{2,1,0:T(8,128)S(1)} %get-tuple-element.25, f32[48,64,144]{2,1,0:T(8,128)S(1)} %get-tuple-element.24, f32[48,64]{1,0:T(8,128)S(1)} %fusion.34), kind=kLoop, calls=%fused_computation.1 | loop fusion | flops 2654208 | bytes 5320704 | tf_op jit(solution)/shard_map/convert_element_type | solution.py:93
  16.5 4.5 %convert_element_type.116 = bf16[48,8,2304]{2,1,0:T(8,128)(2,1)} reshape(bf16[48,64,288]{2,1,0:T(8,128)(2,1)} %fusion) | data formatting | bytes 3538944 | tf_op jit(solution)/shard_map/convert_element_type | solution.py:93
  21.1 3.1 %copy.33 = bf16[48,8,2304]{2,0,1:T(8,128)(2,1)} copy(bf16[48,8,2304]{2,1,0:T(8,128)(2,1)} %convert_element_type.116) | data formatting | bytes 3538944 | tf_op jit(solution)/shard_map/convert_element_type | solution.py:93
  24.5 7.2 %shard_map.87 = (bf16[36,32,512]{2,1,0:T(8,128)(2,1)S(1)}, f32[16,128]{1,0:T(8,128)S(1)}) custom-call(bf16[32,64,288]{2,1,0:T(8,128)(2,1)S(1)} %pad.16.rows, f32[16,128]{1,0:T(8,128)S(1)} %concatenate.38.gain, bf16[288,288]{1,0:T(8,128)(2,1)S(1)} %fusion.32.table), custom_call_target="tpu_custom_call" | custom-call | tf_op jit(solution)/shard_map/pallas_call | solution.py:151
  31.7 1.0 copy-done
  34.0 37.7 %shard_map.88 = (bf16[8,36,32,512]{3,2,1,0:T(8,128)(2,1)}, f32[8,32,128]{2,1,0:T(8,128)}, bf16[8,48,2304]{2,1,0:T(8,128)(2,1)}, s32[8,8,128]{2,1,0:T(8,128)}) custom-call(bf16[36,32,512]{2,1,0:T(8,128)(2,1)} %copy-done, f32[32,128]{1,0:T(8,128)} %select_maximum_fusion.e, bf16[8,48,2304]{2,1,0:T(8,128)(2,1)} %bitcast.58, s32[8,128]{1,0:T(8,128)} %pad.18.lab), custom_call_target="tpu_custom_call" | custom-call | tf_op jit(solution)/shard_map/pallas_call | solution.py:255
  71.7 0.9 slice_reduce_fusion.1
  74.2 2.1 %convolution_convert_fusion = bf16[200,2304]{1,0:T(8,128)(2,1)S(1)} fusion(bf16[384,2304]{1,0:T(8,128)(2,1)} %bitcast.59, s32[384]{0:T(512)S(1)} %eq.56), kind=kOutput, calls=%fused_computation.6 | convolution fusion | flops 354432000 | bytes 2692608 | tf_op jit(solution)/shard_map/dot_general | solution.py:504
  76.3 1.3 reshape.210.sums
  77.7 52.5 %shard_map.89 = (bf16[8,36,32,512]{3,2,1,0:T(8,128)(2,1)}, bf16[8,25,2304]{2,1,0:T(8,128)(2,1)}, f32[8,8,128]{2,1,0:T(8,128)}) custom-call(bf16[8,36,32,512]{3,2,1,0:T(8,128)(2,1)} %get-tuple-element.15.hg_in, bf16[8,25,2304]{2,1,0:T(8,128)(2,1)} %reshape.210.sums, f32[8,8,128]{2,1,0:T(8,128)} %pad.19.den), custom_call_target="tpu_custom_call", output_to_operand_aliasing={{0}: (0, {})} | custom-call | tf_op jit(solution)/shard_map/pallas_call | solution.py:367
  130.2 3.2 %copy.18 = f32[8,25,2304]{2,0,1:T(8,128)} copy(bf16[8,25,2304]{2,1,0:T(8,128)(2,1)} %get-tuple-element.20) | data formatting | bytes 2764800 | tf_op jit(solution)/shard_map/reshape | solution.py:521
  133.4 4.0 %reshape.218 = f32[4,2,25,8,288]{4,3,1,0,2:T(8,128)} reshape(f32[8,25,2304]{2,0,1:T(8,128)} %copy.18) | data formatting | bytes 3686400 | tf_op jit(solution)/shard_map/reshape | solution.py:521
  137.4 2.0 %reduce_sum.20 = f32[2,25,8,288]{3,2,0,1:T(8,128)S(1)} reduce(f32[4,2,25,8,288]{4,3,1,0,2:T(8,128)} %reshape.218, f32[]{:T(128)} %constant.94.clone.1), dimensions={0}, to_apply=%region_0.1 | reduce | flops 345600 | bytes 2304004 | tf_op jit(solution)/shard_map/reduce_sum | solution.py:520
  139.5 1.0 fusion.10
  140.8 9.8 %shard_map.86 = (bf16[36,96,512]{2,1,0:T(8,128)(2,1)S(1)}, f32[24,128]{1,0:T(8,128)}) custom-call(bf16[48,64,288]{2,1,0:T(8,128)(2,1)S(1)} %pad_maximum_fusion.rows, f32[24,128]{1,0:T(8,128)S(1)} %pad_maximum_fusion.1.gain, bf16[288,288]{1,0:T(8,128)(2,1)S(1)} %fusion.32.table), custom_call_target="tpu_custom_call" | custom-call | tf_op jit(solution)/shard_map/pallas_call | solution.py:151
  150.6 9.6 %shard_map.90 = f32[48,128]{1,0:T(8,128)S(1)} custom-call(bf16[36,96,512]{2,1,0:T(8,128)(2,1)S(1)} %get-tuple-element.12.lhs, bf16[8,36,32,512]{3,2,1,0:T(8,128)(2,1)} %get-tuple-element.18.hg, f32[48,256]{1,0:T(8,128)S(1)} %fusion.9.scale), custom_call_target="tpu_custom_call" | custom-call | tf_op jit(solution)/shard_map/pallas_call | solution.py:453
  160.2 0.6 slice_reduce_fusion
  (47 shorter events, 5.0 us)
Async XLA Ops:
  10.2 1.7 %copy-start.5 = (s32[48]{0:T(128)S(1)}, s32[48]{0:T(128)}, u32[]{:S(2)}) copy-start(s32[48]{0:T(128)} %param.11) | copy-start | bytes 580
  12.2 1.3 copy-start.3
  21.1 3.2 %copy-start.1 = (bf16[25,64,288]{2,1,0:T(8,128)(2,1)S(1)}, bf16[25,64,288]{2,1,0:T(8,128)(2,1)}, u32[]{:S(2)}) copy-start(bf16[25,64,288]{2,1,0:T(8,128)(2,1)} %param.8) | copy-start | bytes 2764804
  24.1 9.3 %copy-start.6 = (s32[48]{0:T(128)S(1)}, s32[48]{0:T(128)}, u32[]{:S(2)}) copy-start(s32[48]{0:T(128)} %param.10) | copy-start | bytes 580
  24.1 9.3 %copy-start.7 = (s32[48,1]{0,1:T(1,128)S(1)}, s32[48,1]{0,1:T(1,128)}, u32[]{:S(2)}) copy-start(s32[48,1]{0,1:T(1,128)} %param.9) | copy-start | bytes 580
  31.7 1.0 copy-start
  133.4 6.0 %copy-start.2 = (f32[8,8,128]{2,1,0:T(8,128)S(1)}, f32[8,8,128]{2,1,0:T(8,128)}, u32[]{:S(2)}) copy-start(f32[8,8,128]{2,1,0:T(8,128)} %get-tuple-element.21) | copy-start | bytes 98308
  137.4 3.1 %copy-start.4 = (f32[8,32,128]{2,1,0:T(8,128)S(1)}, f32[8,32,128]{2,1,0:T(8,128)}, u32[]{:S(2)}) copy-start(f32[8,32,128]{2,1,0:T(8,128)} %get-tuple-element.19) | copy-start | bytes 393220

commit v4 on v3

--- a/solution.py
+++ b/solution.py
@@ -94,7 +94,7 @@
     return (contrast, shifted, unrotated)
 
 
-def major_kernel(copies, both, rows, gain, table, out, energy, wide):
+def major_kernel(copies, packed, rows, gain, table, out, energy, wide, dense=None):
     pairs, lanes = gain.shape
     width = table.shape[0]
     turns = width // 2 // copies
@@ -130,8 +130,18 @@
         full = jnp.concatenate(
             [jnp.concatenate(tops, axis=1), jnp.concatenate(ends, axis=1)], axis=0
         )
-        out[m, pl.ds(0, 2 * pairs), :] = full.astype(out.dtype)
-        if both:
+        if packed:
+            main = packed // 8 * 8
+            group = turns // 4
+            start = m // group * out.shape[1]
+            turn = m % group
+            at = pl.multiple_of(start + turn * main, 8)
+            dense[pl.ds(at, main), :] = full[:main]
+            for k in range(main, packed):
+                at = start + group * main + turn * (packed - main) + k - main
+                dense[pl.ds(at, 1), :] = full[k : k + 1]
+        else:
+            out[m, pl.ds(0, 2 * pairs), :] = full.astype(out.dtype)
             tops = [-x for x in tops[half:]] + tops[:half]
             ends = [-x for x in ends[half:]] + ends[:half]
             full = jnp.concatenate(
@@ -140,23 +150,33 @@
             out[m, pl.ds(2 * pairs, 2 * pairs), :] = full.astype(out.dtype)
         return carry
 
+    if packed:
+        dense[...] = jnp.zeros_like(dense)
     lax.fori_loop(0, turns, gather, 0)
-
-
-def rotation_major(rows, gain, table, copies, both):
+    if packed:
+        out[...] = dense[...].reshape(out.shape).astype(out.dtype)
+
+
+def rotation_major(rows, gain, table, copies, packed):
     count, cycles, width = rows.shape
     pairs = count // 2
     turns = width // 2 // copies
     paired = jnp.concatenate([gain[:pairs], gain[pairs:]], axis=1)
+    depth = 2 * copies * cycles
+    scratch = [pltpu.VMEM((width * pairs, 2 * cycles), jnp.float32)]
+    shape = (turns, 2 * count, depth)
+    if packed:
+        shape = (4, -(-(turns // 4 * packed) // 8) * 8, depth)
+        scratch.append(pltpu.VMEM((shape[0] * shape[1], depth), jnp.float32))
     out, energy = pl.pallas_call(
-        functools.partial(major_kernel, copies, both),
+        functools.partial(major_kernel, copies, packed),
         out_shape=(
-            jax.ShapeDtypeStruct((turns, count * (2 if both else 1), 2 * copies * cycles), rows.dtype),
+            jax.ShapeDtypeStruct(shape, rows.dtype),
             jax.ShapeDtypeStruct((pairs, 2 * cycles), jnp.float32),
         ),
         in_specs=[pl.BlockSpec(memory_space=pltpu.VMEM)] * 3,
         out_specs=(pl.BlockSpec(memory_space=pltpu.VMEM),) * 2,
-        scratch_shapes=[pltpu.VMEM((width * pairs, 2 * cycles), jnp.float32)],
+        scratch_shapes=scratch,
         compiler_params=pltpu.CompilerParams(vmem_limit_bytes=32 * 1024 * 1024),
     )(rows, paired, table)
     return out, jnp.concatenate([energy[:, :cycles], energy[:, cycles:]], axis=0)
@@ -414,13 +434,23 @@
     return best
 
 
-def score_kernel(lhs, hg, scale, out, folded, best):
+def score_kernel(per_owner, lhs, hg, scale, out, folded, best):
     step = pl.program_id(0)
-    owners, group, padded, depth = hg.shape
-    rows = lhs.shape[1]
+    owners, _, _, depth = hg.shape
+    group, rows, _ = lhs.shape
     count = rows // 2
+    width = folded.shape[2]
+    main = per_owner // 8 * 8
+    rest = per_owner - main
+    tails = [hg[o, 0, group * main :, :].astype(jnp.float32) for o in range(owners)]
     for g in range(group):
-        block = hg[:, g].reshape(owners * padded, depth)
+        parts = [
+            hg[o, 0, g * main : (g + 1) * main, :].astype(jnp.float32) for o in range(owners)
+        ]
+        parts += [tails[o][g * rest + k : g * rest + k + 1] for o in range(owners) for k in range(rest)]
+        if width > owners * per_owner:
+            parts.append(jnp.zeros((width - owners * per_owner, depth), jnp.float32))
+        block = jnp.concatenate(parts, axis=0).astype(jnp.bfloat16)
         folded[step * group + g] = lax.dot_general(
             lhs[g], block, (((1,), (1,)), ((), ())), preferred_element_type=jnp.float32
         )
@@ -430,7 +460,7 @@
         def tile(t, carry):
             at = pl.ds(pl.multiple_of(t * 8, 8), 8)
             after = pl.ds(pl.multiple_of(count + t * 8, 8), 8)
-            for lane in range(owners * padded // 128):
+            for lane in range(width // 128):
                 cols = pl.ds(lane * 128, 128)
 
                 def take(m):
@@ -445,18 +475,18 @@
         out[...] = jnp.broadcast_to(jnp.max(scores, axis=1, keepdims=True), out.shape)
 
 
-def best_scores(lhs, hg, scale):
+def best_scores(lhs, hg, scale, per_owner):
     turns, rows, depth = lhs.shape
-    owners, _, padded, _ = hg.shape
-    group = 4
-    width = owners * padded
+    owners, pieces, packed, _ = hg.shape
+    width = scale.shape[1]
+    group = turns // pieces
     return pl.pallas_call(
-        score_kernel,
-        grid=(turns // group,),
+        functools.partial(score_kernel, per_owner),
+        grid=(pieces,),
         out_shape=jax.ShapeDtypeStruct((rows // 2, 128), jnp.float32),
         in_specs=[
             pl.BlockSpec((group, rows, depth), lambda i: (i, 0, 0)),
-            pl.BlockSpec((owners, group, padded, depth), lambda i: (0, i, 0, 0)),
+            pl.BlockSpec((owners, 1, packed, depth), lambda i: (0, i, 0, 0)),
             pl.BlockSpec((rows // 2, width), lambda i: (0, 0)),
         ],
         out_specs=pl.BlockSpec((rows // 2, 128), lambda i: (0, 0)),
@@ -481,13 +511,13 @@
     thin = cycle_count // plane
     contrast, shifted, unrotated = prepare(particles, rotation, shifts, defocus)
     table = angle_table(angles).T
-    lhs, _ = rotation_major(shifted, contrast, table, copies, True)
+    lhs, _ = rotation_major(shifted, contrast, table, copies, 0)
     major, energy = rotation_major(
         jnp.pad(references, ((0, padded - per_owner), (0, 0), (0, 0))),
         jnp.ones((padded, cycle_count), jnp.float32),
         table,
         copies,
-        False,
+        per_owner,
     )
     energy = jnp.pad(energy, ((0, 0), (0, -cycle_count % 128)))
     outbox = (
@@ -517,10 +547,14 @@
     all_major, all_sums, all_den = to_owners(
         all_major, sums.reshape(owners, per_owner, thin * row_width), den, owners, fine
     )
-    numerator = jnp.sum(
-        all_sums.astype(jnp.float32).reshape(owners // fine, fine, per_owner, thin, row_width),
-        axis=0,
-    )
+    numerator = lax.optimization_barrier(
+        jnp.sum(
+            all_sums.astype(jnp.float32).reshape(
+                owners // fine, fine, per_owner, thin * row_width
+            ),
+            axis=0,
+        )
+    ).reshape(fine, per_owner, thin, row_width)
     denominator = jnp.sum(
         all_den[:, :thin, :per_owner].reshape(owners // fine, fine, thin, per_owner), axis=0
     ).transpose(0, 2, 1)
@@ -528,17 +562,21 @@
     class_average = class_average.transpose(1, 0, 2, 3).reshape(
         per_owner, fine * thin, row_width
     )
-    power = (
-        jnp.dot(
-            contrast * contrast,
-            all_energy[:, :, :cycle_count].reshape(owners * padded, cycle_count).T,
-            precision=lax.Precision.HIGHEST,
-        )
-        / angles
-    )
-    used = jnp.arange(owners * padded, dtype=jnp.int32) % padded < per_owner
-    scale = jnp.where(used[None, :], 1.0 / (angles * jnp.sqrt(power + EPSILON)), -1.0)
-    return (best_scores(lhs, all_major, scale), class_average)
+    main = per_owner // 8 * 8
+    energies = jnp.concatenate(
+        [
+            all_energy[:, :main, :cycle_count].reshape(-1, cycle_count),
+            all_energy[:, main:per_owner, :cycle_count].reshape(-1, cycle_count),
+        ],
+        axis=0,
+    )
+    power = jnp.dot(contrast * contrast, energies.T, precision=lax.Precision.HIGHEST) / angles
+    scale = jnp.pad(
+        1.0 / (angles * jnp.sqrt(power + EPSILON)),
+        ((0, 0), (0, -owners * per_owner % 128)),
+        constant_values=-1.0,
+    )
+    return (best_scores(lhs, all_major, scale, per_owner), class_average)
 
 
 def solution(mesh):

time: 161 us -> 141 us (0.88)
  Pallas kernels: 117 us -> 101 us
  local copies, waits for them, and re-layouts: 20.5 us -> 16.1 us
    pallas_call x1, Pallas kernels: 52.5 us -> 44.8 us  [to_owners(): pl.pallas_call(functools.partial(owner_kernel, owners, fine), out_shape=(...]
    reshape x2 -> x1, local copies, waits for them, and re-layouts: 7.15 us -> 1.58 us  [on_device(): numerator = lax.optimization_barrier(jnp.sum(all_sums.astype(jnp.float32)...]
    pallas_call x1, Pallas kernels: 37.7 us -> 32.7 us  [spread(): pl.pallas_call(functools.partial(spread_kernel, doms, owners, fine), out_...]
    pallas_call x3, Pallas kernels: 26.6 us -> 23.9 us  [the longest x2 17.4 us: rotation_major(): pl.pallas_call(functools.partial(major_kernel, copies, packed), out_shape...]
where the time goes in v4:
time: 141 us
  Pallas kernels  101 us (72%)
  other arithmetic  17.2 us (12%)
  local copies, waits for them, and re-layouts  16.1 us (11%)
  matrix products  4.96 us (4%)
    pallas_call x1, Pallas kernels, to_owners(): pl.pallas_call(functools.partial(owner_kernel, owners, fine), out_shape=(...  44.8 us
    pallas_call x1, Pallas kernels, spread(): pl.pallas_call(functools.partial(spread_kernel, doms, owners, fine), out_...  32.7 us
    pallas_call x2, Pallas kernels, rotation_major(): pl.pallas_call(functools.partial(major_kernel, copies, packed), out_shape...  17.4 us
    convert_element_type x2, local copies, waits for them, and re-layouts, prepare(): unrotated = (contrast[:, :, None] * turned).astype(jnp.bfloat16)  7.67 us
    pallas_call x1, Pallas kernels, best_scores(): pl.pallas_call(functools.partial(score_kernel, per_owner), grid=(pieces,)...  6.5 us
    another operation x3, other arithmetic  4.88 us
    convert_element_type x1, other arithmetic, prepare(): unrotated = (contrast[:, :, None] * turned).astype(jnp.bfloat16)  2.85 us

profile of v4, /device:TPU:0, one launch (start us, length us, event | category | flops | bytes accessed | tf_op | source)
XLA Modules:
  0.0 140.7 jit_solution(8628561648657667309)
XLA Ops:
  0.7 0.8 convert_bitcast_fusion.1
  1.5 2.8 %multiply_cosine_fusion.1 = (f32[48,8,144]{2,1,0:T(8,128)S(1)}, f32[48,8,144]{2,1,0:T(8,128)S(1)}, f32[48,8,144]{2,1,0:T(8,128)S(1)}, f32[48,8,144]{2,1,0:T(8,128)S(1)}) fusion(f32[48,144]{1,0:T(8,128)S(1)} %add_multiply_fusion, f32[8]{0:T(128)S(1)} %get-tuple-element.45, f32[8]{0:T(128)S(1)} %get-tuple-element.44), kind=kLoop, calls=%fused_computation.27 | loop fusion | flops 110592 | bytes 912448 | tf_op jit(solution)/shard_map/cos | solution.py:56
  4.3 3.7 %fusion.2 = (bf16[48,64,144]{2,1,0:T(8,128)(2,1)S(1)}, bf16[48,64,144]{2,1,0:T(8,128)(2,1)S(1)}) fusion(f32[48,8,144]{2,1,0:T(8,128)S(1)} %get-tuple-element.32, f32[48,8,144]{2,1,0:T(8,128)S(1)} %get-tuple-element.29, f32[48,8,144]{2,1,0:T(8,128)S(1)} %get-tuple-element.33, f32[48,8,144]{2,1,0:T(8,128)S(1)} %get-tuple-element.28, bf16[48,64,288]{2,1,0:T(8,128)(2,1)} %param.7), kind=kLoop, calls=%fused_computation.8 | loop fusion | flops 7077888 | bytes 4423680 | tf_op jit(solution)/shard_map/convert.7
  8.0 0.9 pad_maximum_fusion.rows
  8.9 0.6 negate_convert_fusion
  10.1 1.7 %fusion.10 = f32[48,64,288]{2,1,0:T(8,128)S(1)} fusion(bf16[48,64,288]{2,1,0:T(8,128)(2,1)S(1)} %pad_maximum_fusion.rows, bf16[144,144]{0,1:T(8,128)(2,1)S(1)} %get-tuple-element.47, bf16[144,144]{0,1:T(8,128)(2,1)S(1)} %fusion.20, bf16[144,144]{0,1:T(8,128)(2,1)S(1)} %get-tuple-element.46), kind=kOutput, calls=%fused_computation.31 | convolution fusion | flops 510271488 | bytes 5432832 | tf_op jit(solution)/shard_map/dot_general | solution.py:75
  12.2 1.1 multiply_subtract_fusion
  13.6 2.8 %fusion = bf16[48,64,288]{2,1,0:T(8,128)(2,1)} fusion(f32[48,64,144]{2,1,0:T(8,128)S(1)} %get-tuple-element.25, f32[48,64,144]{2,1,0:T(8,128)S(1)} %get-tuple-element.24, f32[48,64]{1,0:T(8,128)S(1)} %fusion.35), kind=kLoop, calls=%fused_computation.1 | loop fusion | flops 2654208 | bytes 5320704 | tf_op jit(solution)/shard_map/convert_element_type | solution.py:93
  16.4 4.5 %convert_element_type.116 = bf16[48,8,2304]{2,1,0:T(8,128)(2,1)} reshape(bf16[48,64,288]{2,1,0:T(8,128)(2,1)} %fusion) | data formatting | bytes 3538944 | tf_op jit(solution)/shard_map/convert_element_type | solution.py:93
  21.0 3.1 %copy.28 = bf16[48,8,2304]{2,0,1:T(8,128)(2,1)} copy(bf16[48,8,2304]{2,1,0:T(8,128)(2,1)} %convert_element_type.116) | data formatting | bytes 3538944 | tf_op jit(solution)/shard_map/convert_element_type | solution.py:93
  24.5 7.6 %shard_map.87 = (bf16[4,232,512]{2,1,0:T(8,128)(2,1)S(1)}, f32[16,128]{1,0:T(8,128)S(1)}) custom-call(bf16[32,64,288]{2,1,0:T(8,128)(2,1)S(1)} %pad.20.rows, f32[16,128]{1,0:T(8,128)S(1)} %concatenate.41.gain, bf16[288,288]{1,0:T(8,128)(2,1)S(1)} %fusion.33.table), custom_call_target="tpu_custom_call" | custom-call | tf_op jit(solution)/shard_map/pallas_call | solution.py:171
  32.1 0.9 copy-done
  34.4 32.7 %shard_map.88 = (bf16[8,4,232,512]{3,2,1,0:T(8,128)(2,1)}, f32[8,32,128]{2,1,0:T(8,128)}, bf16[8,48,2304]{2,1,0:T(8,128)(2,1)}, s32[8,8,128]{2,1,0:T(8,128)}) custom-call(bf16[4,232,512]{2,1,0:T(8,128)(2,1)} %copy-done, f32[32,128]{1,0:T(8,128)} %select_maximum_fusion.e, bf16[8,48,2304]{2,1,0:T(8,128)(2,1)} %bitcast.48, s32[8,128]{1,0:T(8,128)} %pad.22.lab), custom_call_target="tpu_custom_call" | custom-call | tf_op jit(solution)/shard_map/pallas_call | solution.py:275
  67.1 0.9 slice_reduce_fusion.1
  69.6 2.1 %convolution_convert_fusion = bf16[200,2304]{1,0:T(8,128)(2,1)S(1)} fusion(bf16[384,2304]{1,0:T(8,128)(2,1)} %bitcast.49, s32[384]{0:T(512)S(1)} %eq.54), kind=kOutput, calls=%fused_computation.6 | convolution fusion | flops 354432000 | bytes 2692608 | tf_op jit(solution)/shard_map/dot_general | solution.py:534
  71.7 1.4 %reshape.206.sums = bf16[8,25,2304]{2,1,0:T(8,128)(2,1)} reshape(bf16[200,2304]{1,0:T(8,128)(2,1)S(1)} %convolution_convert_fusion) | data formatting | bytes 1843200 | tf_op jit(solution)/shard_map/reshape | solution.py:548
  73.1 44.8 %shard_map.89 = (bf16[8,4,232,512]{3,2,1,0:T(8,128)(2,1)}, bf16[8,25,2304]{2,1,0:T(8,128)(2,1)}, f32[8,8,128]{2,1,0:T(8,128)}) custom-call(bf16[8,4,232,512]{3,2,1,0:T(8,128)(2,1)} %get-tuple-element.15.hg_in, bf16[8,25,2304]{2,1,0:T(8,128)(2,1)} %reshape.206.sums, f32[8,8,128]{2,1,0:T(8,128)} %pad.23.den), custom_call_target="tpu_custom_call", output_to_operand_aliasing={{0}: (0, {})} | custom-call | tf_op jit(solution)/shard_map/pallas_call | solution.py:387
  118.0 1.5 %convert_reduce_fusion = f32[2,25,2304]{2,1,0:T(8,128)S(1)} fusion(bf16[4,2,25,2304]{3,2,1,0:T(8,128)(2,1)} %bitcast.50), kind=kLoop, calls=%fused_computation.16 | loop fusion | flops 806400 | bytes 1382400 | tf_op jit(solution)/shard_map/reduce_sum | solution.py:551
  119.5 1.1 copy.22
  120.7 1.6 %reshape.212 = f32[2,25,8,288]{3,2,0,1:T(8,128)S(1)} reshape(f32[2,25,2304]{2,0,1:T(2,128)} %copy.22) | data formatting | bytes 921600 | tf_op jit(solution)/shard_map/reshape | solution.py:557
  122.4 1.0 divide_bitcast_fusion
  123.8 9.8 %shard_map.86 = (bf16[36,96,512]{2,1,0:T(8,128)(2,1)S(1)}, f32[24,128]{1,0:T(8,128)}) custom-call(bf16[48,64,288]{2,1,0:T(8,128)(2,1)S(1)} %pad_maximum_fusion.rows, f32[24,128]{1,0:T(8,128)S(1)} %pad_maximum_fusion.1.gain, bf16[288,288]{1,0:T(8,128)(2,1)S(1)} %fusion.33.table), custom_call_target="tpu_custom_call" | custom-call | tf_op jit(solution)/shard_map/pallas_call | solution.py:171
  133.6 6.5 %shard_map.90 = f32[48,128]{1,0:T(8,128)S(1)} custom-call(bf16[36,96,512]{2,1,0:T(8,128)(2,1)S(1)} %get-tuple-element.12.lhs, bf16[8,4,232,512]{3,2,1,0:T(8,128)(2,1)} %get-tuple-element.18.hg, f32[48,256]{1,0:T(8,128)S(1)} %pad.24.scale), custom_call_target="tpu_custom_call" | custom-call | tf_op jit(solution)/shard_map/pallas_call | solution.py:483
  140.1 0.6 slice_reduce_fusion
  (49 shorter events, 5.1 us)
Async XLA Ops:
  10.1 1.7 %copy-start.5 = (s32[48]{0:T(128)S(1)}, s32[48]{0:T(128)}, u32[]{:S(2)}) copy-start(s32[48]{0:T(128)} %param.11) | copy-start | bytes 580
  12.1 1.2 copy-start.4
  21.0 3.3 %copy-start.1 = (bf16[25,64,288]{2,1,0:T(8,128)(2,1)S(1)}, bf16[25,64,288]{2,1,0:T(8,128)(2,1)}, u32[]{:S(2)}) copy-start(bf16[25,64,288]{2,1,0:T(8,128)(2,1)} %param.8) | copy-start | bytes 2764804
  24.1 9.6 %copy-start.6 = (s32[48]{0:T(128)S(1)}, s32[48]{0:T(128)}, u32[]{:S(2)}) copy-start(s32[48]{0:T(128)} %param.10) | copy-start | bytes 580
  24.1 9.6 %copy-start.7 = (s32[48,1]{0,1:T(1,128)S(1)}, s32[48,1]{0,1:T(1,128)}, u32[]{:S(2)}) copy-start(s32[48,1]{0,1:T(1,128)} %param.9) | copy-start | bytes 580
  32.1 0.9 copy-start
  118.0 4.3 %copy-start.3 = (f32[8,8,128]{2,1,0:T(8,128)S(1)}, f32[8,8,128]{2,1,0:T(8,128)}, u32[]{:S(2)}) copy-start(f32[8,8,128]{2,1,0:T(8,128)} %get-tuple-element.21) | copy-start | bytes 98308
  118.0 5.4 %copy-start.2 = (f32[8,32,128]{2,1,0:T(8,128)S(1)}, f32[8,32,128]{2,1,0:T(8,128)}, u32[]{:S(2)}) copy-start(f32[8,32,128]{2,1,0:T(8,128)} %get-tuple-element.19) | copy-start | bytes 393220

commit v5 on v4

--- a/solution.py
+++ b/solution.py
@@ -113,7 +113,7 @@
         wide[pl.ds(i, width, stride=pairs), :] = spectrum
         return carry
 
-    lax.fori_loop(0, pairs, transform, 0)
+    lax.fori_loop(0, pairs, transform, 0, unroll=4)
     low = lax.broadcasted_iota(jnp.int32, (pairs, lanes), 1) < cycles
 
     def gather(m, carry):
@@ -152,7 +152,7 @@
 
     if packed:
         dense[...] = jnp.zeros_like(dense)
-    lax.fori_loop(0, turns, gather, 0)
+    lax.fori_loop(0, turns, gather, 0, unroll=4)
     if packed:
         out[...] = dense[...].reshape(out.shape).astype(out.dtype)
 

time: 141 us -> 132 us (0.936)
  Pallas kernels: 101 us -> 92.1 us
    pallas_call x2, Pallas kernels: 17.4 us -> 8.07 us  [rotation_major(): pl.pallas_call(functools.partial(major_kernel, copies, packed), out_shape...]
where the time goes in v5:
time: 132 us
  Pallas kernels  92.1 us (70%)
  other arithmetic  17.4 us (13%)
  local copies, waits for them, and re-layouts  16.1 us (12%)
  matrix products  4.96 us (4%)
    pallas_call x1, Pallas kernels, to_owners(): pl.pallas_call(functools.partial(owner_kernel, owners, fine), out_shape=(...  44.8 us
    pallas_call x1, Pallas kernels, spread(): pl.pallas_call(functools.partial(spread_kernel, doms, owners, fine), out_...  32.7 us
    pallas_call x2, Pallas kernels, rotation_major(): pl.pallas_call(functools.partial(major_kernel, copies, packed), out_shape...  8.07 us
    convert_element_type x2, local copies, waits for them, and re-layouts, prepare(): unrotated = (contrast[:, :, None] * turned).astype(jnp.bfloat16)  7.67 us
    pallas_call x1, Pallas kernels, best_scores(): pl.pallas_call(functools.partial(score_kernel, per_owner), grid=(pieces,)...  6.5 us
    another operation x3, other arithmetic  5.06 us
    convert_element_type x1, other arithmetic, prepare(): unrotated = (contrast[:, :, None] * turned).astype(jnp.bfloat16)  2.85 us
    cos x1, other arithmetic, phase_turns(): cf, sf = (jnp.cos(fine)[:, None], jnp.sin(fine)[:, None])  2.79 us

profile of v5, /device:TPU:0, one launch (start us, length us, event | category | flops | bytes accessed | tf_op | source)
XLA Modules:
  0.0 131.5 jit_solution(6874187640019661355)
XLA Ops:
  0.7 0.8 convert_bitcast_fusion.1
  1.5 2.8 %multiply_cosine_fusion.1 = (f32[48,8,144]{2,1,0:T(8,128)S(1)}, f32[48,8,144]{2,1,0:T(8,128)S(1)}, f32[48,8,144]{2,1,0:T(8,128)S(1)}, f32[48,8,144]{2,1,0:T(8,128)S(1)}) fusion(f32[48,144]{1,0:T(8,128)S(1)} %add_multiply_fusion, f32[8]{0:T(128)S(1)} %get-tuple-element.45, f32[8]{0:T(128)S(1)} %get-tuple-element.44), kind=kLoop, calls=%fused_computation.27 | loop fusion | flops 110592 | bytes 912448 | tf_op jit(solution)/shard_map/cos | solution.py:56
  4.3 3.9 %fusion.2 = (bf16[48,64,144]{2,1,0:T(8,128)(2,1)S(1)}, bf16[48,64,144]{2,1,0:T(8,128)(2,1)S(1)}) fusion(f32[48,8,144]{2,1,0:T(8,128)S(1)} %get-tuple-element.32, f32[48,8,144]{2,1,0:T(8,128)S(1)} %get-tuple-element.29, f32[48,8,144]{2,1,0:T(8,128)S(1)} %get-tuple-element.33, f32[48,8,144]{2,1,0:T(8,128)S(1)} %get-tuple-element.28, bf16[48,64,288]{2,1,0:T(8,128)(2,1)} %param.7), kind=kLoop, calls=%fused_computation.8 | loop fusion | flops 7077888 | bytes 4423680 | tf_op jit(solution)/shard_map/convert.7
  8.2 0.9 pad_maximum_fusion.rows
  9.1 0.6 negate_convert_fusion
  10.3 1.7 %fusion.10 = f32[48,64,288]{2,1,0:T(8,128)S(1)} fusion(bf16[48,64,288]{2,1,0:T(8,128)(2,1)S(1)} %pad_maximum_fusion.rows, bf16[144,144]{0,1:T(8,128)(2,1)S(1)} %get-tuple-element.47, bf16[144,144]{0,1:T(8,128)(2,1)S(1)} %fusion.20, bf16[144,144]{0,1:T(8,128)(2,1)S(1)} %get-tuple-element.46), kind=kOutput, calls=%fused_computation.31 | convolution fusion | flops 510271488 | bytes 5432832 | tf_op jit(solution)/shard_map/dot_general | solution.py:75
  12.3 1.1 multiply_subtract_fusion
  13.8 2.8 %fusion = bf16[48,64,288]{2,1,0:T(8,128)(2,1)} fusion(f32[48,64,144]{2,1,0:T(8,128)S(1)} %get-tuple-element.25, f32[48,64,144]{2,1,0:T(8,128)S(1)} %get-tuple-element.24, f32[48,64]{1,0:T(8,128)S(1)} %fusion.35), kind=kLoop, calls=%fused_computation.1 | loop fusion | flops 2654208 | bytes 5320704 | tf_op jit(solution)/shard_map/convert_element_type | solution.py:93
  16.6 4.5 %convert_element_type.116 = bf16[48,8,2304]{2,1,0:T(8,128)(2,1)} reshape(bf16[48,64,288]{2,1,0:T(8,128)(2,1)} %fusion) | data formatting | bytes 3538944 | tf_op jit(solution)/shard_map/convert_element_type | solution.py:93
  21.1 3.1 %copy.28 = bf16[48,8,2304]{2,0,1:T(8,128)(2,1)} copy(bf16[48,8,2304]{2,1,0:T(8,128)(2,1)} %convert_element_type.116) | data formatting | bytes 3538944 | tf_op jit(solution)/shard_map/convert_element_type | solution.py:93
  24.6 3.8 %shard_map.87 = (bf16[4,232,512]{2,1,0:T(8,128)(2,1)S(1)}, f32[16,128]{1,0:T(8,128)S(1)}) custom-call(bf16[32,64,288]{2,1,0:T(8,128)(2,1)S(1)} %pad.20.rows, f32[16,128]{1,0:T(8,128)S(1)} %concatenate.41.gain, bf16[288,288]{1,0:T(8,128)(2,1)S(1)} %fusion.33.table), custom_call_target="tpu_custom_call" | custom-call | tf_op jit(solution)/shard_map/pallas_call | solution.py:171
  28.4 0.9 copy-done
  30.7 32.7 %shard_map.88 = (bf16[8,4,232,512]{3,2,1,0:T(8,128)(2,1)}, f32[8,32,128]{2,1,0:T(8,128)}, bf16[8,48,2304]{2,1,0:T(8,128)(2,1)}, s32[8,8,128]{2,1,0:T(8,128)}) custom-call(bf16[4,232,512]{2,1,0:T(8,128)(2,1)} %copy-done, f32[32,128]{1,0:T(8,128)} %select_maximum_fusion.e, bf16[8,48,2304]{2,1,0:T(8,128)(2,1)} %bitcast.48, s32[8,128]{1,0:T(8,128)} %pad.22.lab), custom_call_target="tpu_custom_call" | custom-call | tf_op jit(solution)/shard_map/pallas_call | solution.py:275
  63.4 0.9 slice_reduce_fusion.1
  65.9 2.1 %convolution_convert_fusion = bf16[200,2304]{1,0:T(8,128)(2,1)S(1)} fusion(bf16[384,2304]{1,0:T(8,128)(2,1)} %bitcast.49, s32[384]{0:T(512)S(1)} %eq.54), kind=kOutput, calls=%fused_computation.6 | convolution fusion | flops 354432000 | bytes 2692608 | tf_op jit(solution)/shard_map/dot_general | solution.py:534
  68.0 1.4 %reshape.206.sums = bf16[8,25,2304]{2,1,0:T(8,128)(2,1)} reshape(bf16[200,2304]{1,0:T(8,128)(2,1)S(1)} %convolution_convert_fusion) | data formatting | bytes 1843200 | tf_op jit(solution)/shard_map/reshape | solution.py:548
  69.4 44.8 %shard_map.89 = (bf16[8,4,232,512]{3,2,1,0:T(8,128)(2,1)}, bf16[8,25,2304]{2,1,0:T(8,128)(2,1)}, f32[8,8,128]{2,1,0:T(8,128)}) custom-call(bf16[8,4,232,512]{3,2,1,0:T(8,128)(2,1)} %get-tuple-element.15.hg_in, bf16[8,25,2304]{2,1,0:T(8,128)(2,1)} %reshape.206.sums, f32[8,8,128]{2,1,0:T(8,128)} %pad.23.den), custom_call_target="tpu_custom_call", output_to_operand_aliasing={{0}: (0, {})} | custom-call | tf_op jit(solution)/shard_map/pallas_call | solution.py:387
  114.2 1.5 %convert_reduce_fusion = f32[2,25,2304]{2,1,0:T(8,128)S(1)} fusion(bf16[4,2,25,2304]{3,2,1,0:T(8,128)(2,1)} %bitcast.50), kind=kLoop, calls=%fused_computation.16 | loop fusion | flops 806400 | bytes 1382400 | tf_op jit(solution)/shard_map/reduce_sum | solution.py:551
  115.8 1.1 copy.22
  116.9 1.6 %reshape.212 = f32[2,25,8,288]{3,2,0,1:T(8,128)S(1)} reshape(f32[2,25,2304]{2,0,1:T(2,128)} %copy.22) | data formatting | bytes 921600 | tf_op jit(solution)/shard_map/reshape | solution.py:557
  118.6 1.0 divide_bitcast_fusion
  120.1 4.3 %shard_map.86 = (bf16[36,96,512]{2,1,0:T(8,128)(2,1)S(1)}, f32[24,128]{1,0:T(8,128)}) custom-call(bf16[48,64,288]{2,1,0:T(8,128)(2,1)S(1)} %pad_maximum_fusion.rows, f32[24,128]{1,0:T(8,128)S(1)} %pad_maximum_fusion.1.gain, bf16[288,288]{1,0:T(8,128)(2,1)S(1)} %fusion.33.table), custom_call_target="tpu_custom_call" | custom-call | tf_op jit(solution)/shard_map/pallas_call | solution.py:171
  124.4 6.5 %shard_map.90 = f32[48,128]{1,0:T(8,128)S(1)} custom-call(bf16[36,96,512]{2,1,0:T(8,128)(2,1)S(1)} %get-tuple-element.12.lhs, bf16[8,4,232,512]{3,2,1,0:T(8,128)(2,1)} %get-tuple-element.18.hg, f32[48,256]{1,0:T(8,128)S(1)} %pad.24.scale), custom_call_target="tpu_custom_call" | custom-call | tf_op jit(solution)/shard_map/pallas_call | solution.py:483
  130.9 0.6 slice_reduce_fusion
  (49 shorter events, 5.1 us)
Async XLA Ops:
  10.3 1.7 %copy-start.5 = (s32[48]{0:T(128)S(1)}, s32[48]{0:T(128)}, u32[]{:S(2)}) copy-start(s32[48]{0:T(128)} %param.11) | copy-start | bytes 580
  12.3 1.2 copy-start.4
  21.1 3.3 %copy-start.1 = (bf16[25,64,288]{2,1,0:T(8,128)(2,1)S(1)}, bf16[25,64,288]{2,1,0:T(8,128)(2,1)}, u32[]{:S(2)}) copy-start(bf16[25,64,288]{2,1,0:T(8,128)(2,1)} %param.8) | copy-start | bytes 2764804
  24.3 5.7 %copy-start.6 = (s32[48]{0:T(128)S(1)}, s32[48]{0:T(128)}, u32[]{:S(2)}) copy-start(s32[48]{0:T(128)} %param.10) | copy-start | bytes 580
  24.3 5.7 %copy-start.7 = (s32[48,1]{0,1:T(1,128)S(1)}, s32[48,1]{0,1:T(1,128)}, u32[]{:S(2)}) copy-start(s32[48,1]{0,1:T(1,128)} %param.9) | copy-start | bytes 580
  28.4 0.9 copy-start
  114.2 4.3 %copy-start.3 = (f32[8,8,128]{2,1,0:T(8,128)S(1)}, f32[8,8,128]{2,1,0:T(8,128)}, u32[]{:S(2)}) copy-start(f32[8,8,128]{2,1,0:T(8,128)} %get-tuple-element.21) | copy-start | bytes 98308
  114.2 5.4 %copy-start.2 = (f32[8,32,128]{2,1,0:T(8,128)S(1)}, f32[8,32,128]{2,1,0:T(8,128)}, u32[]{:S(2)}) copy-start(f32[8,32,128]{2,1,0:T(8,128)} %get-tuple-element.19) | copy-start | bytes 393220

commit v6 on v5

--- a/solution.py
+++ b/solution.py
@@ -248,18 +248,18 @@
         ended.append((sent, remote(src, dst.at[source], send, recv, *to)))
 
     part = pl.ds(piece, quarter)
+    for i in range(1, lines):
+        to = (c + i * fine) % owners
+        source = (c + owners - i * fine) % owners
+        sent = remote(h.at[part], hg.at[c, part], s1.at[i], r1.at[i], d, to)
+        sent.start()
+        ended.append((sent, remote(h.at[part], hg.at[source, part], s1.at[i], r1.at[i], d, to)))
     for i in range(1, plane):
         other = (slab + i) % plane
         source = (slab + plane - i) % plane
         to = (other // fine, first + other % fine)
         move(lab, lg, slab, source, sl.at[i], rl.at[i], to)
         move(u.at[other], ug, slab, source, su.at[i], ru.at[i], to)
-    for i in range(1, lines):
-        to = (c + i * fine) % owners
-        source = (c + owners - i * fine) % owners
-        sent = remote(h.at[part], hg.at[c, part], s1.at[i], r1.at[i], d, to)
-        sent.start()
-        ended.append((sent, remote(h.at[part], hg.at[source, part], s1.at[i], r1.at[i], d, to)))
     for i in range(1, owners):
         to = (c + i) % owners
         move(e, eg, c, (c + owners - i) % owners, se.at[i], re.at[i], (d, to))
@@ -328,6 +328,9 @@
     def to_mate(source, k):
         send(source, source, here, there, (sm.at[k], rm.at[k]), (mate, c))
 
+    waiting = []
+    for line in range(1, lines):
+        waiting.append((shard(0, line), line, to_across(shard(0, line), line)))
     from_side = []
     for col in range(1, fine):
         to = (d, c - c % fine + (c % fine + col) % fine)
@@ -348,9 +351,6 @@
                     ),
                 )
             )
-    waiting = []
-    for line in range(1, lines):
-        waiting.append((shard(0, line), line, to_across(shard(0, line), line)))
     for i in range(1, owners):
         to = (c + i) % owners
         source = (c + owners - i) % owners

time: 132 us -> 132 us (level)
  no operation moved by 1% of the time
where the time goes in v6:
time: 132 us
  Pallas kernels  92.1 us (70%)
  other arithmetic  17.4 us (13%)
  local copies, waits for them, and re-layouts  16.1 us (12%)
  matrix products  4.96 us (4%)
    pallas_call x1, Pallas kernels, to_owners(): pl.pallas_call(functools.partial(owner_kernel, owners, fine), out_shape=(...  44.8 us
    pallas_call x1, Pallas kernels, spread(): pl.pallas_call(functools.partial(spread_kernel, doms, owners, fine), out_...  32.7 us
    pallas_call x2, Pallas kernels, rotation_major(): pl.pallas_call(functools.partial(major_kernel, copies, packed), out_shape...  8.08 us
    convert_element_type x2, local copies, waits for them, and re-layouts, prepare(): unrotated = (contrast[:, :, None] * turned).astype(jnp.bfloat16)  7.67 us
    pallas_call x1, Pallas kernels, best_scores(): pl.pallas_call(functools.partial(score_kernel, per_owner), grid=(pieces,)...  6.5 us
    another operation x3, other arithmetic  5.06 us
    convert_element_type x1, other arithmetic, prepare(): unrotated = (contrast[:, :, None] * turned).astype(jnp.bfloat16)  2.85 us
    cos x1, other arithmetic, phase_turns(): cf, sf = (jnp.cos(fine)[:, None], jnp.sin(fine)[:, None])  2.79 us

profile of v6, /device:TPU:0, one launch (start us, length us, event | category | flops | bytes accessed | tf_op | source)
XLA Modules:
  0.0 131.5 jit_solution(14953809912195241039)
XLA Ops:
  0.7 0.8 convert_bitcast_fusion.1
  1.5 2.8 %multiply_cosine_fusion.1 = (f32[48,8,144]{2,1,0:T(8,128)S(1)}, f32[48,8,144]{2,1,0:T(8,128)S(1)}, f32[48,8,144]{2,1,0:T(8,128)S(1)}, f32[48,8,144]{2,1,0:T(8,128)S(1)}) fusion(f32[48,144]{1,0:T(8,128)S(1)} %add_multiply_fusion, f32[8]{0:T(128)S(1)} %get-tuple-element.45, f32[8]{0:T(128)S(1)} %get-tuple-element.44), kind=kLoop, calls=%fused_computation.27 | loop fusion | flops 110592 | bytes 912448 | tf_op jit(solution)/shard_map/cos | solution.py:56
  4.3 3.9 %fusion.2 = (bf16[48,64,144]{2,1,0:T(8,128)(2,1)S(1)}, bf16[48,64,144]{2,1,0:T(8,128)(2,1)S(1)}) fusion(f32[48,8,144]{2,1,0:T(8,128)S(1)} %get-tuple-element.32, f32[48,8,144]{2,1,0:T(8,128)S(1)} %get-tuple-element.29, f32[48,8,144]{2,1,0:T(8,128)S(1)} %get-tuple-element.33, f32[48,8,144]{2,1,0:T(8,128)S(1)} %get-tuple-element.28, bf16[48,64,288]{2,1,0:T(8,128)(2,1)} %param.7), kind=kLoop, calls=%fused_computation.8 | loop fusion | flops 7077888 | bytes 4423680 | tf_op jit(solution)/shard_map/convert.7
  8.2 0.9 pad_maximum_fusion.rows
  9.1 0.6 negate_convert_fusion
  10.3 1.7 %fusion.10 = f32[48,64,288]{2,1,0:T(8,128)S(1)} fusion(bf16[48,64,288]{2,1,0:T(8,128)(2,1)S(1)} %pad_maximum_fusion.rows, bf16[144,144]{0,1:T(8,128)(2,1)S(1)} %get-tuple-element.47, bf16[144,144]{0,1:T(8,128)(2,1)S(1)} %fusion.20, bf16[144,144]{0,1:T(8,128)(2,1)S(1)} %get-tuple-element.46), kind=kOutput, calls=%fused_computation.31 | convolution fusion | flops 510271488 | bytes 5432832 | tf_op jit(solution)/shard_map/dot_general | solution.py:75
  12.3 1.1 multiply_subtract_fusion
  13.8 2.8 %fusion = bf16[48,64,288]{2,1,0:T(8,128)(2,1)} fusion(f32[48,64,144]{2,1,0:T(8,128)S(1)} %get-tuple-element.25, f32[48,64,144]{2,1,0:T(8,128)S(1)} %get-tuple-element.24, f32[48,64]{1,0:T(8,128)S(1)} %fusion.35), kind=kLoop, calls=%fused_computation.1 | loop fusion | flops 2654208 | bytes 5320704 | tf_op jit(solution)/shard_map/convert_element_type | solution.py:93
  16.6 4.5 %convert_element_type.116 = bf16[48,8,2304]{2,1,0:T(8,128)(2,1)} reshape(bf16[48,64,288]{2,1,0:T(8,128)(2,1)} %fusion) | data formatting | bytes 3538944 | tf_op jit(solution)/shard_map/convert_element_type | solution.py:93
  21.1 3.1 %copy.28 = bf16[48,8,2304]{2,0,1:T(8,128)(2,1)} copy(bf16[48,8,2304]{2,1,0:T(8,128)(2,1)} %convert_element_type.116) | data formatting | bytes 3538944 | tf_op jit(solution)/shard_map/convert_element_type | solution.py:93
  24.6 3.8 %shard_map.87 = (bf16[4,232,512]{2,1,0:T(8,128)(2,1)S(1)}, f32[16,128]{1,0:T(8,128)S(1)}) custom-call(bf16[32,64,288]{2,1,0:T(8,128)(2,1)S(1)} %pad.20.rows, f32[16,128]{1,0:T(8,128)S(1)} %concatenate.41.gain, bf16[288,288]{1,0:T(8,128)(2,1)S(1)} %fusion.33.table), custom_call_target="tpu_custom_call" | custom-call | tf_op jit(solution)/shard_map/pallas_call | solution.py:171
  28.4 0.9 copy-done
  30.7 32.7 %shard_map.88 = (bf16[8,4,232,512]{3,2,1,0:T(8,128)(2,1)}, f32[8,32,128]{2,1,0:T(8,128)}, bf16[8,48,2304]{2,1,0:T(8,128)(2,1)}, s32[8,8,128]{2,1,0:T(8,128)}) custom-call(bf16[4,232,512]{2,1,0:T(8,128)(2,1)} %copy-done, f32[32,128]{1,0:T(8,128)} %select_maximum_fusion.e, bf16[8,48,2304]{2,1,0:T(8,128)(2,1)} %bitcast.48, s32[8,128]{1,0:T(8,128)} %pad.22.lab), custom_call_target="tpu_custom_call" | custom-call | tf_op jit(solution)/shard_map/pallas_call | solution.py:275
  63.4 0.9 slice_reduce_fusion.1
  65.9 2.1 %convolution_convert_fusion = bf16[200,2304]{1,0:T(8,128)(2,1)S(1)} fusion(bf16[384,2304]{1,0:T(8,128)(2,1)} %bitcast.49, s32[384]{0:T(512)S(1)} %eq.54), kind=kOutput, calls=%fused_computation.6 | convolution fusion | flops 354432000 | bytes 2692608 | tf_op jit(solution)/shard_map/dot_general | solution.py:534
  68.0 1.4 %reshape.206.sums = bf16[8,25,2304]{2,1,0:T(8,128)(2,1)} reshape(bf16[200,2304]{1,0:T(8,128)(2,1)S(1)} %convolution_convert_fusion) | data formatting | bytes 1843200 | tf_op jit(solution)/shard_map/reshape | solution.py:548
  69.4 44.8 %shard_map.89 = (bf16[8,4,232,512]{3,2,1,0:T(8,128)(2,1)}, bf16[8,25,2304]{2,1,0:T(8,128)(2,1)}, f32[8,8,128]{2,1,0:T(8,128)}) custom-call(bf16[8,4,232,512]{3,2,1,0:T(8,128)(2,1)} %get-tuple-element.15.hg_in, bf16[8,25,2304]{2,1,0:T(8,128)(2,1)} %reshape.206.sums, f32[8,8,128]{2,1,0:T(8,128)} %pad.23.den), custom_call_target="tpu_custom_call", output_to_operand_aliasing={{0}: (0, {})} | custom-call | tf_op jit(solution)/shard_map/pallas_call | solution.py:387
  114.2 1.5 %convert_reduce_fusion = f32[2,25,2304]{2,1,0:T(8,128)S(1)} fusion(bf16[4,2,25,2304]{3,2,1,0:T(8,128)(2,1)} %bitcast.50), kind=kLoop, calls=%fused_computation.16 | loop fusion | flops 806400 | bytes 1382400 | tf_op jit(solution)/shard_map/reduce_sum | solution.py:551
  115.8 1.1 copy.22
  116.9 1.6 %reshape.212 = f32[2,25,8,288]{3,2,0,1:T(8,128)S(1)} reshape(f32[2,25,2304]{2,0,1:T(2,128)} %copy.22) | data formatting | bytes 921600 | tf_op jit(solution)/shard_map/reshape | solution.py:557
  118.6 1.0 divide_bitcast_fusion
  120.1 4.3 %shard_map.86 = (bf16[36,96,512]{2,1,0:T(8,128)(2,1)S(1)}, f32[24,128]{1,0:T(8,128)}) custom-call(bf16[48,64,288]{2,1,0:T(8,128)(2,1)S(1)} %pad_maximum_fusion.rows, f32[24,128]{1,0:T(8,128)S(1)} %pad_maximum_fusion.1.gain, bf16[288,288]{1,0:T(8,128)(2,1)S(1)} %fusion.33.table), custom_call_target="tpu_custom_call" | custom-call | tf_op jit(solution)/shard_map/pallas_call | solution.py:171
  124.4 6.5 %shard_map.90 = f32[48,128]{1,0:T(8,128)S(1)} custom-call(bf16[36,96,512]{2,1,0:T(8,128)(2,1)S(1)} %get-tuple-element.12.lhs, bf16[8,4,232,512]{3,2,1,0:T(8,128)(2,1)} %get-tuple-element.18.hg, f32[48,256]{1,0:T(8,128)S(1)} %pad.24.scale), custom_call_target="tpu_custom_call" | custom-call | tf_op jit(solution)/shard_map/pallas_call | solution.py:483
  130.9 0.6 slice_reduce_fusion
  (49 shorter events, 5.1 us)
Async XLA Ops:
  10.3 1.7 %copy-start.5 = (s32[48]{0:T(128)S(1)}, s32[48]{0:T(128)}, u32[]{:S(2)}) copy-start(s32[48]{0:T(128)} %param.11) | copy-start | bytes 580
  12.3 1.2 copy-start.4
  21.1 3.3 %copy-start.1 = (bf16[25,64,288]{2,1,0:T(8,128)(2,1)S(1)}, bf16[25,64,288]{2,1,0:T(8,128)(2,1)}, u32[]{:S(2)}) copy-start(bf16[25,64,288]{2,1,0:T(8,128)(2,1)} %param.8) | copy-start | bytes 2764804
  24.3 5.7 %copy-start.6 = (s32[48]{0:T(128)S(1)}, s32[48]{0:T(128)}, u32[]{:S(2)}) copy-start(s32[48]{0:T(128)} %param.10) | copy-start | bytes 580
  24.3 5.7 %copy-start.7 = (s32[48,1]{0,1:T(1,128)S(1)}, s32[48,1]{0,1:T(1,128)}, u32[]{:S(2)}) copy-start(s32[48,1]{0,1:T(1,128)} %param.9) | copy-start | bytes 580
  28.4 0.9 copy-start
  114.2 4.3 %copy-start.3 = (f32[8,8,128]{2,1,0:T(8,128)S(1)}, f32[8,8,128]{2,1,0:T(8,128)}, u32[]{:S(2)}) copy-start(f32[8,8,128]{2,1,0:T(8,128)} %get-tuple-element.21) | copy-start | bytes 98308
  114.2 5.4 %copy-start.2 = (f32[8,32,128]{2,1,0:T(8,128)S(1)}, f32[8,32,128]{2,1,0:T(8,128)}, u32[]{:S(2)}) copy-start(f32[8,32,128]{2,1,0:T(8,128)} %get-tuple-element.19) | copy-start | bytes 393220
